TPU v7x, 128 devices: a whole 4x4x4 slice. The times are simulated.
128 devices in a mesh: gy: 8 (over z_lo, x), gz: 16 (over y, z_hi, core).
Axes of the slice: x: 4, y: 4, z: 4 (z_hi: 2, z_lo: 2; z = z_hi * 2 + z_lo), core: 2. Of those that a mesh axis runs over, the one named last changes fastest.
Arguments:
- density: float32 [1024, 128, 256], P('gy', 'gz'), may hold values from 0.5 to 2
- momentum: float32 [3, 1024, 128, 256], P(None, 'gy', 'gz'), may hold values from -3 to 3
- energy: float32 [1024, 128, 256], P('gy', 'gz'), may hold values from 2 to 4
- wall_operator: float32 [1024, 1024], replicated, may hold values from -0.1875 to 0.1875
- span_operator: float32 [128, 128], replicated, may hold values from -0.5 to 0.5
- damping: float32 [1024], replicated, may hold values from 0.1 to 1
Outputs:
- new_density: float32 [1024, 128, 256], P('gy', 'gz')
- new_momentum: float32 [3, 1024, 128, 256], P(None, 'gy', 'gz')
- new_energy: float32 [1024, 128, 256], P('gy', 'gz')
All inputs are finite; a program needn't handle non-finite values.
Results may differ from a plain program's by a relative error of at most 0.00009.
Values sent between devices are 32-bit elements; how exact they have to be, the bound alone decides.
A program may use at most 256 MiB of HBM per device.

v0:
```python
import jax
import jax.numpy as jnp
from jax import lax
from jax.sharding import PartitionSpec as P

gamma_less = 0.4
time_step = 0.1


def with_halo(cells, sides, width, closed):
    for axis, dim in sides:
        count = lax.axis_size(axis)
        ends = count if closed else count - 1
        head = lax.slice_in_dim(cells, 0, width, axis=dim)
        tail = lax.slice_in_dim(cells, cells.shape[dim] - width, cells.shape[dim], axis=dim)
        cells = jnp.concatenate(
            [
                lax.ppermute(tail, axis, [(i, (i + 1) % count) for i in range(ends)]),
                cells,
                lax.ppermute(head, axis, [((i + 1) % count, i) for i in range(ends)]),
            ],
            axis=dim,
        )
    return cells


def flux_along(conserved, direction):
    velocity = conserved[1 + direction] / conserved[0]
    kinetic = (
        0.5
        * (conserved[1] * conserved[1] + conserved[2] * conserved[2] + conserved[3] * conserved[3])
        / conserved[0]
    )
    pressure = gamma_less * (conserved[4] - kinetic)
    components = [conserved[1 + direction]]
    for column in range(3):
        product = conserved[1 + column] * velocity
        if column == direction:
            product = product + pressure
        components.append(product)
    components.append((conserved[4] + pressure) * velocity)
    return jnp.stack(components)


def x_derivative(flux_field):
    widths = [(0, 0)] * (flux_field.ndim - 1) + [(2, 2)]
    padded = jnp.pad(flux_field, widths, mode="edge")
    return (
        8.0 * (padded[..., 3:-1] - padded[..., 1:-3]) - (padded[..., 4:] - padded[..., :-4])
    ) / 12.0


def fourth_difference(padded, along_axis, length_out):

    def shifted(offset):
        return lax.slice_in_dim(padded, offset, offset + length_out, axis=along_axis)

    return shifted(0) - 4.0 * shifted(1) + 6.0 * shifted(2) - 4.0 * shifted(3) + shifted(4)


def local(density, momentum, energy, wall_operator, span_operator, damping):
    conserved = jnp.concatenate([density[None], momentum, energy[None]], axis=0)
    rows_here = conserved.shape[1]
    planes_here = conserved.shape[2]
    first_row = lax.axis_index("gy") * rows_here
    local_damping = lax.dynamic_slice_in_dim(damping, first_row, rows_here)
    along_x = x_derivative(flux_along(conserved, 0))
    upward = flux_along(conserved, 1)
    sideways = flux_along(conserved, 2)
    derivative = jnp.einsum(
        "ij,fjzx->fizx",
        wall_operator,
        lax.all_to_all(upward, "gy", split_axis=3, concat_axis=1, tiled=True),
        precision=lax.Precision.HIGHEST,
    )
    deriv_y = lax.all_to_all(derivative, "gy", split_axis=1, concat_axis=3, tiled=True)
    derivative = jnp.einsum(
        "ij,fyjx->fyix",
        span_operator,
        lax.all_to_all(sideways, "gz", split_axis=3, concat_axis=2, tiled=True),
        precision=lax.Precision.HIGHEST,
    )
    deriv_z = lax.all_to_all(derivative, "gz", split_axis=2, concat_axis=3, tiled=True)
    near_y = with_halo(conserved, (("gy", 1),), 2, False)
    near_z = with_halo(conserved, (("gz", 2),), 2, True)
    smoothing = fourth_difference(near_y, 1, rows_here) + fourth_difference(near_z, 2, planes_here)
    tendency = -along_x - deriv_y - deriv_z - local_damping[None, :, None, None] * smoothing
    advanced = conserved + time_step * tendency
    return (advanced[0], advanced[1:4], advanced[4])


def solution(mesh):
    in_specs = (P("gy", "gz", None), P(None, "gy", "gz", None), P("gy", "gz", None), P(), P(), P())
    out_specs = (P("gy", "gz", None), P(None, "gy", "gz", None), P("gy", "gz", None))
    return jax.shard_map(local, mesh=mesh, in_specs=in_specs, out_specs=out_specs, check_vma=False)
```

profile of v0, /device:TPU:87, one launch (start us, length us, event | category | flops | bytes accessed | tf_op | source)
XLA Modules:
  0.0 498.6 jit_solution(11741611885511762760)
XLA Ops:
  0.6 2.7 copy.70
  3.3 2.6 copy.71
  5.9 2.6 copy.72
  8.6 1.5 bitcast_dynamic-update-slice_fusion.3
  11.9 2.3 copy-done.7
  14.2 2.3 copy-done.8
  16.5 2.7 copy.81
  19.2 5.3 %all-to-all-start = ((f32[5,128,8,256]{1,2,0,3:T(8,128)}), f32[5,128,8,256]{1,2,0,3:T(8,128)}, u32[]{:S(2)}, u32[]{:S(2)}) async-start(f32[5,128,8,256]{1,2,0,3:T(8,128)} %copy.81), calls=%async_computation | async-start | bytes 10485760 | tf_op jit(solution)/shard_map/all_to_all | solution.py:73
  24.5 5.1 %copy.89 = f32[5,128,8,256]{1,2,0,3:T(8,128)} copy(f32[5,128,8,256]{1,2,3,0:T(8,128)} %copy-done.8) | data formatting | bytes 10485760 | tf_op jit(solution)/shard_map/stack | solution.py:42
  29.7 71.1 %all-to-all-done = f32[5,128,8,256]{1,2,0,3:T(8,128)} async-done(((f32[5,128,8,256]{1,2,0,3:T(8,128)}), f32[5,128,8,256]{1,2,0,3:T(8,128)}, u32[]{:S(2)}, u32[]{:S(2)}) %all-to-all-start) | async-done | bytes 5242912 | tf_op jit(solution)/shard_map/all_to_all | solution.py:73
  100.8 8.7 %all-to-all-start.2 = ((f32[5,128,8,256]{1,2,0,3:T(8,128)}), f32[5,128,8,256]{1,2,0,3:T(8,128)}, u32[]{:S(2)}, u32[]{:S(2)}) async-start(f32[5,128,8,256]{1,2,0,3:T(8,128)} %copy.89), calls=%async_computation.2 | async-start | bytes 10485760 | tf_op jit(solution)/shard_map/all_to_all | solution.py:80
  109.5 7.9 %copy.83 = f32[5,8,128,8,32]{2,1,4,3,0:T(8,128)} copy(f32[5,8,128,8,32]{2,3,0,4,1:T(8,128)} %bitcast.17) | data formatting | bytes 10485760 | tf_op jit(solution)/shard_map/all_to_all | solution.py:73
  117.4 6.8 %all_to_all.55 = f32[5,1024,8,32]{1,3,2,0:T(8,128)} reshape(f32[5,8,128,8,32]{2,1,4,3,0:T(8,128)} %copy.83) | data formatting | bytes 10485760 | tf_op jit(solution)/shard_map/all_to_all | solution.py:73
  124.2 22.0 %fusion.25 = f32[5,1024,8,32]{1,3,2,0:T(8,128)} fusion(f32[5,1024,8,32]{1,3,2,0:T(8,128)} %all_to_all.55, f32[1024,1024]{1,0:T(8,128)} %param.9), kind=kOutput, calls=%fused_computation.42 | convolution fusion | flops 16106127360 | bytes 14680064 | tf_op jit(solution)/shard_map/ij,fjzx->fizx/dot_general | solution.py:70
  146.1 13.3 %copy.84 = f32[5,1024,8,32]{3,2,0,1:T(8,128)} copy(f32[5,1024,8,32]{1,3,2,0:T(8,128)} %fusion.25) | data formatting | bytes 10485760 | tf_op jit(solution)/shard_map/ij,fjzx->fizx/transpose | solution.py:70
  159.4 14.8 %reshape.21 = f32[8,1,163840]{2,1,0:T(1,128)} reshape(f32[1024,5,8,32]{3,2,1,0:T(8,128)} %bitcast.138) | data formatting | bytes 10485760
  174.2 15.9 %all-to-all-done.2 = f32[5,128,8,256]{1,2,0,3:T(8,128)} async-done(((f32[5,128,8,256]{1,2,0,3:T(8,128)}), f32[5,128,8,256]{1,2,0,3:T(8,128)}, u32[]{:S(2)}, u32[]{:S(2)}) %all-to-all-start.2) | async-done | bytes 5242912 | tf_op jit(solution)/shard_map/all_to_all | solution.py:80
  190.1 16.9 %all-to-all-start.1 = ((f32[8,1,163840]{2,1,0:T(1,128)}), f32[8,1,163840]{2,1,0:T(1,128)}, u32[]{:S(2)}, u32[]{:S(2)}) async-start(f32[8,1,163840]{2,1,0:T(1,128)} %reshape.21), calls=%async_computation.1 | async-start | bytes 10485760 | tf_op jit(solution)/shard_map/all_to_all | solution.py:76
  207.0 3.7 copy.91
  210.7 11.4 %fusion.28 = f32[5,128,128,16]{2,1,3,0:T(8,128)} fusion(f32[5,128,128,16]{1,3,2,0:T(8,128)S(1)} %bitcast.150, f32[128,128]{1,0:T(8,128)S(1)} %copy-done), kind=kOutput, calls=%fused_computation.43 | convolution fusion | flops 2013265920 | bytes 10551296 | tf_op jit(solution)/shard_map/ij,fyjx->fyix/dot_general | solution.py:77
  222.1 6.1 %copy.93 = f32[5,128,128,16]{1,3,0,2:T(8,128)} copy(f32[5,128,128,16]{2,1,3,0:T(8,128)} %fusion.28) | data formatting | bytes 10485760 | tf_op jit(solution)/shard_map/ij,fyjx->fyix/transpose | solution.py:77
  228.2 56.2 %all-to-all-done.1 = f32[8,1,163840]{2,1,0:T(1,128)} async-done(((f32[8,1,163840]{2,1,0:T(1,128)}), f32[8,1,163840]{2,1,0:T(1,128)}, u32[]{:S(2)}, u32[]{:S(2)}) %all-to-all-start.1) | async-done | bytes 5242912 | tf_op jit(solution)/shard_map/all_to_all | solution.py:76
  284.4 8.1 %all-to-all-start.3 = ((f32[5,128,128,16]{1,3,0,2:T(8,128)}), f32[5,128,128,16]{1,3,0,2:T(8,128)}, u32[]{:S(2)}, u32[]{:S(2)}) async-start(f32[5,128,128,16]{1,3,0,2:T(8,128)} %copy.93), calls=%async_computation.3 | async-start | bytes 10485760 | tf_op jit(solution)/shard_map/all_to_all | solution.py:83
  292.6 1.9 pad_maximum_fusion.4
  294.5 2.3 fusion.43
  296.8 1.2 collective-permute-start.2
  298.0 5.6 %fusion.42 = (f32[5,2,8,256]{1,2,3,0:T(8,128)}, f32[5,2,8,256]{1,2,3,0:T(8,128)}) fusion(f32[5,128,8,256]{1,2,3,0:T(8,128)S(1)} %pad_maximum_fusion.4), kind=kLoop, calls=%fused_computation.88 | loop fusion | bytes 327680 | tf_op jit(solution)/shard_map/slice | solution.py:15
  303.5 3.3 copy.99
  306.8 1.9 collective-permute-start.1
  308.7 3.3 copy.97
  312.1 5.5 %collective-permute-start = (f32[5,2,8,256]{3,2,1,0:T(8,128)S(1)}, f32[5,2,8,256]{3,2,1,0:T(8,128)}, u32[]{:S(2)}, u32[]{:S(2)}) collective-permute-start(f32[5,2,8,256]{3,2,1,0:T(8,128)S(1)} %copy.97), channel_id=1, source_target_pairs={{0,16},{16,32},{32,48},{48,64},{64,80},{80,96},{96,112},{1,17},{17... | collective-permute-start | bytes 245768 | tf_op jit(solution)/shard_map/ppermute | solution.py:18
  317.5 0.8 slice_bitcast_fusion.3
  318.3 0.8 dynamic_slice.3
  319.1 3.9 copy.98
  323.0 3.1 copy.100
  326.1 14.6 %maximum_maximum_fusion = (f32[5,130,8,256]{1,2,3,0:T(8,128)}, f32[5,130,8,256]{1,2,3,0:T(8,128)}) fusion(f32[1,128,8,256]{1,2,3,0:T(8,128)} %bitcast.145, f32[3,128,8,256]{1,2,3,0:T(8,128)S(1)} %copy.72, f32[1,128,8,256]{1,2,3,0:T(8,128)} %bitcast.141, f32[5,2,8,256]{1,2,3,0:T(8,128)} %copy.98, f32[5,2,8,256]{1,2,3,0:T(8,128)} %copy.100), kind=kLoop, calls=%fused_computation | loop fusion | flops 7987200 | bytes 16056320 | tf_op jit(solution)/shard_map/concatenate | solution.py:16
  340.7 23.0 %collective-permute-done.2 = f32[5,128,2,256]{1,2,3,0:T(2,128)} collective-permute-done((f32[5,128,2,256]{1,2,3,0:T(2,128)}, f32[5,128,2,256]{1,2,3,0:T(2,128)}, u32[]{:S(2)}, u32[]{:S(2)}) %collective-permute-start.2) | collective-permute-done | bytes 1310752 | tf_op jit(solution)/shard_map/ppermute | solution.py:18
  363.7 24.3 %collective-permute-done.3 = f32[5,128,2,256]{1,2,3,0:T(2,128)} collective-permute-done((f32[5,128,2,256]{1,2,3,0:T(2,128)}, f32[5,128,2,256]{1,2,3,0:T(2,128)}, u32[]{:S(2)}, u32[]{:S(2)}) %collective-permute-start.3) | collective-permute-done | bytes 1310752 | tf_op jit(solution)/shard_map/ppermute | solution.py:20
  388.0 8.9 %maximum_maximum_fusion.1 = (f32[5,128,10,256]{1,2,3,0:T(8,128)}, f32[5,128,10,256]{1,2,3,0:T(8,128)}) fusion(f32[1,128,8,256]{1,2,3,0:T(8,128)S(1)} %bitcast.147, f32[3,128,8,256]{1,2,3,0:T(8,128)S(1)} %copy.72, f32[1,128,8,256]{1,2,3,0:T(8,128)S(1)} %bitcast.142, f32[5,128,2,256]{1,2,3,0:T(2,128)} %collective-permute-done.2, ...), kind=kLoop, calls=%fused_computation.2 | loop fusion | flops 9830400 | bytes 20971520 | tf_op jit(solution)/shard_map/concatenate | solution.py:16
  397.5 16.8 %reduce = f32[8,163840]{1,0:T(8,128)} reduce(f32[8,1,163840]{2,1,0:T(1,128)} %all-to-all-done.1, f32[]{:T(128)} %broadcast.28), dimensions={1}, to_apply=%all_to_all.56.reduce_sub_computation | reduce | bytes 10485764 | tf_op jit(solution)/shard_map/all_to_all | solution.py:76
  414.3 16.3 %reshape.22 = f32[1024,5,8,32]{3,2,1,0:T(8,128)} reshape(f32[8,163840]{1,0:T(8,128)} %reduce) | data formatting | bytes 10485760
  430.6 14.0 %copy.109 = f32[5,128,8,8,32]{1,2,4,3,0:T(8,128)} copy(f32[5,128,8,8,32]{4,2,0,1,3:T(8,128)} %bitcast.139) | data formatting | bytes 10485760 | tf_op jit(solution)/shard_map/all_to_all | solution.py:76
  444.6 5.6 %copy.95 = f32[5,128,8,16,16]{1,4,3,2,0:T(8,128)} copy(f32[5,128,8,16,16]{1,4,0,2,3:T(8,128)} %bitcast.39) | data formatting | bytes 10485760 | tf_op jit(solution)/shard_map/all_to_all | solution.py:83
  450.2 37.2 %fusion.10 = f32[5,128,8,256]{1,2,3,0:T(8,128)} fusion(f32[5,128,8,256]{1,2,3,0:T(8,128)} %bitcast.149, f32[5,128,8,2]{1,2,3,0:T(8,128)S(1)} %reshape.18, f32[5,128,8,256]{1,2,3,0:T(8,128)} %copy-done.7, f32[5,128,8,2]{1,2,3,0:T(8,128)S(1)} %reshape.17, f32[5,128,10,256]{1,2,3,0:T(8,128)} %get-tuple-element.27, f32[5,128,10,256]{1,2,3,0:T(8,128)} %get-tuple-element.26, ...), kind=kLoop, calls=%fused_computation.18 | loop fusion | flops 41943040 | bytes 68239872 | tf_op jit(solution)/shard_map/add | solution.py:88
  487.5 3.2 slice_bitcast_fusion
  490.6 2.4 copy.102
  493.0 2.6 copy.103
  495.6 2.6 copy.101
  (33 shorter events, 2.3 us)
Async XLA Ops:
  0.6 210.1 %copy-start = (f32[128,128]{1,0:T(8,128)S(1)}, f32[128,128]{1,0:T(8,128)}, u32[]{:S(2)}) copy-start(f32[128,128]{1,0:T(8,128)} %param.10) | copy-start | bytes 196612
  8.6 1.8 copy-start.2
  8.6 1.8 copy-start.5
  11.9 2.3 copy-start.7
  14.2 2.3 copy-start.8
  19.2 81.6 %all-to-all-start = ((f32[5,128,8,256]{1,2,0,3:T(8,128)}), f32[5,128,8,256]{1,2,0,3:T(8,128)}, u32[]{:S(2)}, u32[]{:S(2)}) async-start(f32[5,128,8,256]{1,2,0,3:T(8,128)} %copy.81), calls=%async_computation | async-start | bytes 10485760 | tf_op jit(solution)/shard_map/all_to_all | solution.py:73
  100.8 89.3 %all-to-all-start.2 = ((f32[5,128,8,256]{1,2,0,3:T(8,128)}), f32[5,128,8,256]{1,2,0,3:T(8,128)}, u32[]{:S(2)}, u32[]{:S(2)}) async-start(f32[5,128,8,256]{1,2,0,3:T(8,128)} %copy.89), calls=%async_computation.2 | async-start | bytes 10485760 | tf_op jit(solution)/shard_map/all_to_all | solution.py:80
  190.1 94.4 %all-to-all-start.1 = ((f32[8,1,163840]{2,1,0:T(1,128)}), f32[8,1,163840]{2,1,0:T(1,128)}, u32[]{:S(2)}, u32[]{:S(2)}) async-start(f32[8,1,163840]{2,1,0:T(1,128)} %reshape.21), calls=%async_computation.1 | async-start | bytes 10485760 | tf_op jit(solution)/shard_map/all_to_all | solution.py:76
  284.4 160.1 %all-to-all-start.3 = ((f32[5,128,128,16]{1,3,0,2:T(8,128)}), f32[5,128,128,16]{1,3,0,2:T(8,128)}, u32[]{:S(2)}, u32[]{:S(2)}) async-start(f32[5,128,128,16]{1,3,0,2:T(8,128)} %copy.93), calls=%async_computation.3 | async-start | bytes 10485760 | tf_op jit(solution)/shard_map/all_to_all | solution.py:83
  296.8 66.9 %collective-permute-start.2 = (f32[5,128,2,256]{1,2,3,0:T(2,128)}, f32[5,128,2,256]{1,2,3,0:T(2,128)}, u32[]{:S(2)}, u32[]{:S(2)}) collective-permute-start(f32[5,128,2,256]{1,2,3,0:T(2,128)} %get-tuple-element.28), channel_id=1, source_target_pairs={{0,1},{1,2},{2,3},{3,4},{4,5},{5,6},{6,7},{7,8},{8,9},{9,10},{10,1... | collective-permute-start | bytes 3932168 | tf_op jit(solution)/shard_map/ppermute | solution.py:18
  297.9 90.1 %collective-permute-start.3 = (f32[5,128,2,256]{1,2,3,0:T(2,128)}, f32[5,128,2,256]{1,2,3,0:T(2,128)}, u32[]{:S(2)}, u32[]{:S(2)}) collective-permute-start(f32[5,128,2,256]{1,2,3,0:T(2,128)} %get-tuple-element.29), channel_id=1, source_target_pairs={{1,0},{2,1},{3,2},{4,3},{5,4},{6,5},{7,6},{8,7},{9,8},{10,9},{11,1... | collective-permute-start | bytes 3932168 | tf_op jit(solution)/shard_map/ppermute | solution.py:20
  306.8 16.1 %collective-permute-start.1 = (f32[5,2,8,256]{3,2,1,0:T(8,128)S(1)}, f32[5,2,8,256]{3,2,1,0:T(8,128)S(1)}, u32[]{:S(2)}, u32[]{:S(2)}) collective-permute-start(f32[5,2,8,256]{3,2,1,0:T(8,128)S(1)} %copy.99), channel_id=1, source_target_pairs={{16,0},{32,16},{48,32},{64,48},{80,64},{96,80},{112,96},{17,1},{33... | collective-permute-start | bytes 245768 | tf_op jit(solution)/shard_map/ppermute | solution.py:20
  312.1 7.0 %collective-permute-start = (f32[5,2,8,256]{3,2,1,0:T(8,128)S(1)}, f32[5,2,8,256]{3,2,1,0:T(8,128)}, u32[]{:S(2)}, u32[]{:S(2)}) collective-permute-start(f32[5,2,8,256]{3,2,1,0:T(8,128)S(1)} %copy.97), channel_id=1, source_target_pairs={{0,16},{16,32},{32,48},{48,64},{64,80},{80,96},{96,112},{1,17},{17... | collective-permute-start | bytes 245768 | tf_op jit(solution)/shard_map/ppermute | solution.py:18
  326.1 61.9 %copy-start.3 = (f32[128,8,256]{0,1,2:T(8,128)S(1)}, f32[128,8,256]{0,1,2:T(8,128)}, u32[]{:S(2)}) copy-start(f32[128,8,256]{0,1,2:T(8,128)} %copy.70) | copy-start | bytes 3145732
  326.1 61.9 %copy-start.6 = (f32[128,8,256]{0,1,2:T(8,128)S(1)}, f32[128,8,256]{0,1,2:T(8,128)}, u32[]{:S(2)}) copy-start(f32[128,8,256]{0,1,2:T(8,128)} %copy.71) | copy-start | bytes 3145732
  444.6 5.7 %copy-start.4 = (f32[128,8,256]{0,1,2:T(8,128)S(1)}, f32[128,8,256]{0,1,2:T(8,128)}, u32[]{:S(2)}) copy-start(f32[128,8,256]{0,1,2:T(8,128)} %copy.70) | copy-start | bytes 3145732
  487.5 3.2 slice-start
  490.6 7.7 %copy-start.1 = (f32[128,128]{1,0:T(8,128)S(1)}, f32[128,128]{1,0:T(8,128)}, u32[]{:S(2)}) copy-start(f32[128,128]{1,0:T(8,128)} %param.10) | copy-start | bytes 196612
where the time goes:
time: 506 us; the launch traced here: 499 us
  waiting for transfers between devices  191 us (38%)
  local copies, waits for them, and re-layouts  143 us (28%)
  other arithmetic  82.7 us (16%)
  starting transfers between devices  47.6 us (9%)
  matrix products  33.4 us (7%)
    all_to_all x1, waiting for transfers between devices, local(): lax.all_to_all(upward, 'gy', split_axis=3, concat_axis=1, tiled=True)  71.1 us
    all_to_all x1, waiting for transfers between devices, local(): lax.all_to_all(derivative, 'gy', split_axis=1, concat_axis=3, tiled=True)  56.2 us
    unnamed x27, local copies, waits for them, and re-layouts  51.3 us
    add x1, other arithmetic, local(): advanced = conserved + time_step * tendency  37.2 us
    ppermute x2, waiting for transfers between devices, with_halo(): lax.ppermute(head, axis, [((i + 1) % count, i) for i in range(ends)])  24.3 us
    concatenate x2, other arithmetic, with_halo(): jnp.concatenate([lax.ppermute(tail, axis, [(i, (i + 1) % count) for i in...  23.5 us
    ppermute x2, waiting for transfers between devices, with_halo(): lax.ppermute(tail, axis, [(i, (i + 1) % count) for i in range(ends)])  23 us
    dot_general x1, matrix products, local(): jnp.einsum('ij,fjzx->fizx', wall_operator, lax.all_to_all(upward, 'gy', s...  22 us
  transfers between devices with their start and end apart: 8, of which 5 were waited for; matrix products, arithmetic and copies ran while one was open for 36% of the time, Pallas kernels for 0%

commit v1 on v0

v1 whole, which is shorter than its diff:
```python
import functools

import jax
import jax.numpy as jnp
import numpy as np
from jax import lax
from jax.experimental import pallas as pl
from jax.experimental.pallas import tpu as pltpu
from jax.sharding import PartitionSpec as P

MESH = pl.DeviceIdType.MESH
GAMMA_LESS = 0.4
TIME_STEP = 0.1
GY, GZ = 8, 16
ROWS, PLANES, CELLS, LANES = 128, 8, 256, 128
NY, NZ = GY * ROWS, GZ * PLANES
HOLD = ROWS // GZ
PAD = 8


def flux_along(c, direction):
    inverse = 1.0 / c[0]
    velocity = c[1 + direction] * inverse
    kinetic = 0.5 * (c[1] * c[1] + c[2] * c[2] + c[3] * c[3]) * inverse
    pressure = GAMMA_LESS * (c[4] - kinetic)
    out = [c[1 + direction]]
    for column in range(3):
        product = c[1 + column] * velocity
        if column == direction:
            product = product + pressure
        out.append(product)
    out.append((c[4] + pressure) * velocity)
    return out


def split(x):
    high = x.astype(jnp.bfloat16)
    low = (x - high.astype(jnp.float32)).astype(jnp.bfloat16)
    return high, low


def dot(a, b):
    return jnp.dot(a, b, preferred_element_type=jnp.float32)


def exchange(
    dens, mom, ene, wall, span, damp, damp_rows, fourth,
    dy_out, dz_out,
    own, lines_y, lines_z, by_plane, dy_send, dz_send, wall_f, wall_h, wall_l, flux_h, flux_l, span_3,
    ysend, yrecv, zsend, zrecv, ysend2, yrecv2, zsend2, zrecv2, local_sem,
):
    gy = lax.axis_index("gy")
    gz = lax.axis_index("gz")
    y_peers = [(lax.rem(gy + d, GY), gz) for d in range(1, GY)]
    z_peers = [(gy, lax.rem(gz + d, GZ)) for d in range(1, GZ)]

    loads = []
    for h in range(2):
        lanes = pl.ds(h * LANES, LANES)
        loads += [
            pltpu.make_async_copy(dens.at[:, lanes], own.at[h, 0], local_sem.at[3 * h]),
            pltpu.make_async_copy(mom.at[:, :, lanes], own.at[h, pl.ds(1, 3)], local_sem.at[3 * h + 1]),
            pltpu.make_async_copy(ene.at[:, lanes], own.at[h, 4], local_sem.at[3 * h + 2]),
        ]
    load_wall = pltpu.make_async_copy(wall, wall_f, local_sem.at[6])
    for copy in loads:
        copy.start()
    load_wall.start()

    barrier = pltpu.get_barrier_semaphore()
    for peer in y_peers + z_peers:
        pl.semaphore_signal(barrier, inc=1, device_id=peer, device_id_type=MESH)
    for copy in loads:
        copy.wait()

    @pl.loop(0, 5)
    def _(f):
        for p in range(PLANES):
            for h in range(2):
                by_plane[p, h, f] = own[h, f, pl.ds(p, ROWS, stride=PLANES), :]

    pl.semaphore_wait(barrier, GY + GZ - 2)

    y_out = []
    for d in range(1, GY):
        peer = y_peers[d - 1]
        y_out.append(
            pltpu.make_async_remote_copy(
                by_plane.at[peer[0]],
                lines_y.at[:, :, pl.ds(PAD + gy * ROWS, ROWS), :],
                ysend.at[d - 1], yrecv.at[d - 1], device_id=peer, device_id_type=MESH,
            )
        )
    z_out = []
    for d in range(1, GZ):
        peer = z_peers[d - 1]
        z_out.append(
            pltpu.make_async_remote_copy(
                own.at[:, :, pl.ds(peer[1] * (HOLD * PLANES), HOLD * PLANES), :],
                lines_z.at[gz],
                zsend.at[d - 1], zrecv.at[d - 1], device_id=peer, device_id_type=MESH,
            )
        )
    for copy in y_out:
        copy.start()
    for copy in z_out:
        copy.start()
    keep = [
        pltpu.make_async_copy(by_plane.at[gy], lines_y.at[:, :, pl.ds(PAD + gy * ROWS, ROWS), :], local_sem.at[4]),
        pltpu.make_async_copy(own.at[:, :, pl.ds(gz * (HOLD * PLANES), HOLD * PLANES), :], lines_z.at[gz], local_sem.at[5]),
    ]
    for copy in keep:
        copy.start()

    load_wall.wait()

    @pl.loop(0, NY // 64)
    def _(i):
        rows = pl.ds(i * 64, 64)
        high, low = split(wall_f[rows, :])
        wall_h[rows, :] = high
        wall_l[rows, :] = low

    high, low = split(span[...])
    span_3[:, 0:NZ] = high
    span_3[:, NZ : 2 * NZ] = high
    span_3[:, 2 * NZ : 3 * NZ] = low
    for h in range(2):
        for f in range(5):
            lines_y[h, f, 0:PAD, :] = jnp.zeros((PAD, LANES), jnp.float32)
            lines_y[h, f, PAD + NY : 2 * PAD + NY, :] = jnp.zeros((PAD, LANES), jnp.float32)

    keep[0].wait()
    for copy in y_out:
        copy.wait_recv()

    for h in range(2):

        @pl.loop(0, NY // 64)
        def _(i):
            r = pl.multiple_of(i * 64, 64)
            c = [lines_y[h, f, pl.ds(PAD + r, 64), :] for f in range(5)]
            for f, value in enumerate(flux_along(c, 1)):
                high, low = split(value)
                flux_h[pl.ds(r, 64), f * LANES : (f + 1) * LANES] = high
                flux_l[pl.ds(r, 64), f * LANES : (f + 1) * LANES] = low

        @pl.loop(0, GY)
        def _(g):
            r = pl.multiple_of(g * ROWS, ROWS)
            rows = pl.ds(r, ROWS)
            total = dot(wall_h[rows, :], flux_h[...])
            total += dot(wall_h[rows, :], flux_l[...])
            total += dot(wall_l[rows, :], flux_h[...])
            weight = damp_rows[rows, :]
            for f in range(5):
                window = lines_y[h, f, pl.ds(r, ROWS + 2 * PAD), :]

                def at(k, window=window):
                    return window[PAD + k : PAD + k + ROWS]

                smooth = at(-2) - 4.0 * at(-1) + 6.0 * at(0) - 4.0 * at(1) + at(2)
                dy_send[g, h, f] = total[:, f * LANES : (f + 1) * LANES] + weight * smooth

    y_back = []
    for d in range(1, GY):
        peer = y_peers[d - 1]
        y_back.append(
            pltpu.make_async_remote_copy(
                dy_send.at[peer[0]], dy_out.at[gy],
                ysend2.at[d - 1], yrecv2.at[d - 1], device_id=peer, device_id_type=MESH,
            )
        )
        y_back[-1].start()
    keep_y = pltpu.make_async_copy(dy_send.at[gy], dy_out.at[gy], local_sem.at[0])
    keep_y.start()

    keep[1].wait()
    for copy in z_out:
        copy.wait_recv()

    @pl.loop(0, HOLD)
    def _(r):
        at = pl.ds(pl.multiple_of(r * PLANES, PLANES), PLANES)
        weight = damp[gy * ROWS + gz * HOLD + r]
        for h in range(2):
            c = [lines_z[:, h, f, at, :].reshape(NZ, LANES) for f in range(5)]
            high, low = split(jnp.concatenate(flux_along(c, 2), axis=1))
            total = dot(span_3[...], jnp.concatenate([high, low, high], axis=0))
            high, low = split(jnp.concatenate(c, axis=1))
            total += weight * dot(fourth[...], jnp.concatenate([high, low], axis=0))
            for f in range(5):
                dz_send[:, h, f, at, :] = total[:, f * LANES : (f + 1) * LANES].reshape(GZ, PLANES, LANES)

    z_back = []
    for d in range(1, GZ):
        peer = z_peers[d - 1]
        z_back.append(
            pltpu.make_async_remote_copy(
                dz_send.at[peer[1]], dz_out.at[:, :, pl.ds(gz * (HOLD * PLANES), HOLD * PLANES), :],
                zsend2.at[d - 1], zrecv2.at[d - 1], device_id=peer, device_id_type=MESH,
            )
        )
        z_back[-1].start()
    keep_z = pltpu.make_async_copy(
        dz_send.at[gz], dz_out.at[:, :, pl.ds(gz * (HOLD * PLANES), HOLD * PLANES), :], local_sem.at[1]
    )
    keep_z.start()
    keep_y.wait()
    keep_z.wait()
    for copy in y_out + z_out:
        copy.wait_send()
    for copy in y_back + z_back:
        copy.wait()


def finish(dens, mom, ene, dy, dz, shift, new_dens, new_mom, new_ene, turned):
    c = [dens[...], mom[0], mom[1], mom[2], ene[...]]
    count = dens.shape[0] // PLANES
    for h in range(2):
        for f in range(5):
            for p in range(PLANES):
                turned[h, f, pl.ds(p, count, stride=PLANES), :] = dy[p, h, f]
    for f, value in enumerate(flux_along(c, 0)):
        high, low = split(value)
        along = (dot(high, shift[...]) + dot(low, shift[...])) * (1.0 / 12.0)
        across = jnp.concatenate([turned[h, f] + dz[h, f] for h in range(2)], axis=1)
        value = c[f] - TIME_STEP * (along + across)
        if f == 0:
            new_dens[...] = value
        elif f == 4:
            new_ene[...] = value
        else:
            new_mom[f - 1] = value


def fourth_matrix():
    m = np.zeros((NZ, NZ), np.float32)
    for i in range(NZ):
        for k, w in ((-2, 1.0), (-1, -4.0), (0, 6.0), (1, -4.0), (2, 1.0)):
            m[i, (i + k) % NZ] += w
    return np.concatenate([m, m], axis=1)


def shift_matrix():
    m = np.zeros((CELLS, CELLS), np.float32)
    for i in range(CELLS):
        for k, w in ((1, 8.0), (-1, -8.0), (2, -1.0), (-2, 1.0)):
            m[min(max(i + k, 0), CELLS - 1), i] += w
    return m


ANY = pl.BlockSpec(memory_space=pl.ANY)
VMEM = pl.BlockSpec(memory_space=pltpu.VMEM)
DMA = pltpu.SemaphoreType.DMA


def local(density, momentum, energy, wall_operator, span_operator, damping):
    cells = ROWS * PLANES
    dens = density.reshape(cells, CELLS)
    mom = momentum.reshape(3, cells, CELLS)
    ene = energy.reshape(cells, CELLS)
    f32, bf16 = jnp.float32, jnp.bfloat16
    dy, dz = pl.pallas_call(
        exchange,
        out_shape=(
            jax.ShapeDtypeStruct((PLANES, 2, 5, ROWS, LANES), f32),
            jax.ShapeDtypeStruct((2, 5, cells, LANES), f32),
        ),
        in_specs=[ANY, ANY, ANY, ANY, VMEM, pl.BlockSpec(memory_space=pltpu.SMEM), VMEM, VMEM],
        out_specs=(ANY, ANY),
        scratch_shapes=[
            pltpu.VMEM((2, 5, cells, LANES), f32),
            pltpu.VMEM((2, 5, NY + 2 * PAD, LANES), f32),
            pltpu.VMEM((GZ, 2, 5, HOLD * PLANES, LANES), f32),
            pltpu.VMEM((PLANES, 2, 5, ROWS, LANES), f32),
            pltpu.VMEM((GY, 2, 5, ROWS, LANES), f32),
            pltpu.VMEM((GZ, 2, 5, HOLD * PLANES, LANES), f32),
            pltpu.VMEM((NY, NY), f32),
            pltpu.VMEM((NY, NY), bf16),
            pltpu.VMEM((NY, NY), bf16),
            pltpu.VMEM((NY, 5 * LANES), bf16),
            pltpu.VMEM((NY, 5 * LANES), bf16),
            pltpu.VMEM((NZ, 3 * NZ), bf16),
            DMA((GY - 1,)), DMA((GY - 1,)), DMA((GZ - 1,)), DMA((GZ - 1,)),
            DMA((GY - 1,)), DMA((GY - 1,)), DMA((GZ - 1,)), DMA((GZ - 1,)),
            DMA((7,)),
        ],
        compiler_params=pltpu.CompilerParams(
            collective_id=0, has_side_effects=True, vmem_limit_bytes=62 << 20
        ),
        name="exchange",
    )(
        dens, mom, ene, wall_operator, span_operator, damping,
        jnp.broadcast_to(damping[:, None], (NY, LANES)),
        jnp.asarray(fourth_matrix(), bf16),
    )
    steps = 16
    block = cells // steps
    field = pl.BlockSpec((block, CELLS), lambda i: (i, 0))
    three = pl.BlockSpec((3, block, CELLS), lambda i: (0, i, 0))
    five = pl.BlockSpec((2, 5, block, LANES), lambda i: (0, 0, i, 0))
    new = pl.pallas_call(
        finish,
        grid=(steps,),
        out_shape=(
            jax.ShapeDtypeStruct((cells, CELLS), f32),
            jax.ShapeDtypeStruct((3, cells, CELLS), f32),
            jax.ShapeDtypeStruct((cells, CELLS), f32),
        ),
        in_specs=[
            field, three, field,
            pl.BlockSpec((PLANES, 2, 5, ROWS // steps, LANES), lambda i: (0, 0, 0, i, 0)),
            five,
            pl.BlockSpec((CELLS, CELLS), lambda i: (0, 0)),
        ],
        out_specs=(field, three, field),
        scratch_shapes=[pltpu.VMEM((2, 5, block, LANES), f32)],
        name="finish",
    )(dens, mom, ene, dy, dz, jnp.asarray(shift_matrix(), bf16))
    shape = (ROWS, PLANES, CELLS)
    return new[0].reshape(shape), new[1].reshape((3,) + shape), new[2].reshape(shape)


def solution(mesh):
    in_specs = (P("gy", "gz", None), P(None, "gy", "gz", None), P("gy", "gz", None), P(), P(), P())
    out_specs = (P("gy", "gz", None), P(None, "gy", "gz", None), P("gy", "gz", None))
    return jax.shard_map(local, mesh=mesh, in_specs=in_specs, out_specs=out_specs, check_vma=False)
```

time: 506 us -> 263 us (0.52)
  the two profiles are of different devices: /device:TPU:87 before, /device:TPU:1 now
where the time goes in v1:
time: 263 us; the launch traced here: 259 us
  Pallas kernels  257 us (98%)
    pallas_call x1, Pallas kernels, local(): pl.pallas_call(exchange, out_shape=(jax.ShapeDtypeStruct((PLANES, 2, 5, R...  242 us
    pallas_call x1, Pallas kernels, local(): pl.pallas_call(finish, grid=(steps,), out_shape=(jax.ShapeDtypeStruct((ce...  15.2 us

profile of v1, /device:TPU:1, one launch (start us, length us, event | category | flops | bytes accessed | tf_op | source)
XLA Modules:
  0.0 259.0 jit_solution(10903328170845240808)
XLA Ops:
  0.6 1.7 broadcast_in_dim.2.damp_rows
  2.3 241.6 %exchange.1 = (f32[8,2,5,128,128]{4,3,2,1,0:T(8,128)}, f32[2,5,1024,128]{3,2,1,0:T(8,128)}) custom-call(f32[1024,256]{1,0:T(8,128)} %bitcast.8, f32[3,1024,256]{2,1,0:T(8,128)} %bitcast.6, f32[1024,256]{1,0:T(8,128)} %bitcast.10, f32[1024,1024]{1,0:T(8,128)} %wall.1, f32[128,128]{1,0:T(8,128)} %span.1, f32[1024]{0:T(1024)} %damp.1, ...), custom_call_target="tpu_custom_call" | custom-call | tf_op jit(solution)/shard_map/exchange/pallas_call | solution.py:264
  243.9 15.2 %finish.1 = (f32[1024,256]{1,0:T(8,128)}, f32[3,1024,256]{2,1,0:T(8,128)}, f32[1024,256]{1,0:T(8,128)}) custom-call(f32[1024,256]{1,0:T(8,128)} %bitcast.9, f32[3,1024,256]{2,1,0:T(8,128)} %bitcast.7, f32[1024,256]{1,0:T(8,128)} %bitcast.11, f32[8,2,5,128,128]{4,3,2,1,0:T(8,128)} %get-tuple-element.8.dy, f32[2,5,1024,128]{3,2,1,0:T(8,128)} %get-tuple-element.9.dz, ...), custom_call_target="tpu_custom_call" | custom-call | tf_op jit(solution)/shard_map/finish/pallas_call | solution.py:303

commit v2 on v1

v2 whole, which is shorter than its diff:
```python
import functools

import jax
import jax.numpy as jnp
import numpy as np
from jax import lax
from jax.experimental import pallas as pl
from jax.experimental.pallas import tpu as pltpu
from jax.sharding import PartitionSpec as P

MESH = pl.DeviceIdType.MESH
GAMMA_LESS = 0.4
TIME_STEP = 0.1
GY, GZ = 8, 16
ROWS, PLANES, CELLS, LANES = 128, 8, 256, 128
NY, NZ = GY * ROWS, GZ * PLANES
HOLD = 16
CHUNKS = 4
HALF = NY // 2
PAD = 8


def flux_along(c, direction):
    inverse = 1.0 / c[0]
    velocity = c[1 + direction] * inverse
    kinetic = 0.5 * (c[1] * c[1] + c[2] * c[2] + c[3] * c[3]) * inverse
    pressure = GAMMA_LESS * (c[4] - kinetic)
    out = [c[1 + direction]]
    for column in range(3):
        product = c[1 + column] * velocity
        if column == direction:
            product = product + pressure
        out.append(product)
    out.append((c[4] + pressure) * velocity)
    return out


def split(x):
    high = x.astype(jnp.bfloat16)
    low = (x - high.astype(jnp.float32)).astype(jnp.bfloat16)
    return high, low


def dot(a, b):
    return jnp.dot(a, b, preferred_element_type=jnp.float32)


def exchange(
    dens, mom, ene, wall, span, damp, damp_rows, fourth, order_in, order_out, shift,
    dy_out, dz_out, base_out, near, far,
    own, apart, lines_y, lines_z, dy_send, dz_send, wall_f, wall_h, wall_l, flux_h, flux_l, span_3,
    z1s, z1r, z2s, z2r, x1s, x1r, x2s, x2r, x3s, x3r, y1s, y1r, y2s, y2r, y3s, y3r, load_sem, keep_sem,
):
    gy = lax.axis_index("gy")
    gz = lax.axis_index("gz")
    z_lo, x = gy // 4, lax.rem(gy, 4)
    y, z_hi, core = gz // 4, lax.rem(gz // 2, 2), lax.rem(gz, 2)
    slot = y * 2 + core
    pair = ((1 - z_lo) * 4 + x, gz)
    relay = ((1 - z_lo) * 4 + x, y * 4 + (1 - z_hi) * 2 + core)
    x_of = [lax.rem(x + d, 4) for d in range(4)]
    x_peers = [(z_lo * 4 + other, gz) for other in x_of]
    slot_of = [lax.rem(slot + d, 8) for d in range(8)]
    y_peers = [(gy, (other // 2) * 4 + z_hi * 2 + lax.rem(other, 2)) for other in slot_of]
    far_gz = y * 4 + (1 - z_hi) * 2 + core
    near_row = PAD + gy * ROWS
    far_row = PAD + pair[0] * ROWS

    def send(src, dst, ssem, rsem, peer):
        return pltpu.make_async_remote_copy(src, dst, ssem, rsem, device_id=peer, device_id_type=MESH)

    loads = []
    for h in range(2):
        lanes = pl.ds(h * LANES, LANES)
        loads += [
            pltpu.make_async_copy(dens.at[:, lanes], own.at[h, 0], load_sem.at[3 * h]),
            pltpu.make_async_copy(mom.at[:, :, lanes], own.at[h, pl.ds(1, 3)], load_sem.at[3 * h + 1]),
            pltpu.make_async_copy(ene.at[:, lanes], own.at[h, 4], load_sem.at[3 * h + 2]),
        ]
    load_wall = pltpu.make_async_copy(wall.at[pl.ds(z_lo * HALF, HALF), :], wall_f, load_sem.at[6])
    for copy in loads:
        copy.start()
    load_wall.start()

    barrier = pltpu.get_barrier_semaphore()
    for peer in [pair, relay] + x_peers[1:] + y_peers[1:]:
        pl.semaphore_signal(barrier, inc=1, device_id=peer, device_id_type=MESH)

    z1 = [send(apart.at[u], near.at[u], z1s.at[u], z1r.at[u], pair) for u in range(CHUNKS)]
    z2 = [send(near.at[u], far.at[u], z2s.at[u], z2r.at[u], relay) for u in range(CHUNKS)]
    x1, x2, x3, keeps = [], [], [], []
    for u in range(CHUNKS):
        for copies, source, row, ssem, rsem in ((x1, apart, near_row, x1s, x1r), (x2, near, far_row, x2s, x2r)):
            target = lines_y.at[u, :, pl.ds(row, ROWS), :]
            copies.append(
                [
                    send(source.at[u, x_of[d]], target, ssem.at[u, d - 1], rsem.at[u, d - 1], x_peers[d])
                    for d in range(1, 4)
                ]
            )
        x3.append(
            [
                send(dy_send.at[u, x_of[d]], dy_out.at[u, x], x3s.at[u, d - 1], x3r.at[u, d - 1], x_peers[d])
                for d in range(1, 4)
            ]
        )
        keeps.append(
            [
                pltpu.make_async_copy(apart.at[u, x], lines_y.at[u, :, pl.ds(near_row, ROWS), :], keep_sem.at[u, 0]),
                pltpu.make_async_copy(near.at[u, x], lines_y.at[u, :, pl.ds(far_row, ROWS), :], keep_sem.at[u, 1]),
                pltpu.make_async_copy(
                    apart.at[u, :, :, pl.ds(slot * HOLD, HOLD), :], lines_z.at[u, gz], keep_sem.at[u, 2]
                ),
                pltpu.make_async_copy(
                    far.at[u, :, :, pl.ds(slot * HOLD, HOLD), :], lines_z.at[u, far_gz], keep_sem.at[u, 3]
                ),
                pltpu.make_async_copy(dy_send.at[u, x], dy_out.at[u, x], keep_sem.at[u, 4]),
            ]
        )
    y1, y2, y3, keep_dz = [], [], [], []
    for u in range(CHUNKS):
        for copies, source, index, ssem, rsem in ((y1, apart, gz, y1s, y1r), (y2, far, far_gz, y2s, y2r)):
            copies.append(
                [
                    send(
                        source.at[u, :, :, pl.ds(slot_of[d] * HOLD, HOLD), :], lines_z.at[u, index],
                        ssem.at[u, d - 1], rsem.at[u, d - 1], y_peers[d],
                    )
                    for d in range(1, 8)
                ]
            )
    for h in range(2):
        home = dz_out.at[pl.ds(2 * h, 2), :, :, pl.ds(slot * HOLD, HOLD), :]
        y3.append(
            [
                send(dz_send.at[h, :, slot_of[d]], home, y3s.at[h, d - 1], y3r.at[h, d - 1], y_peers[d])
                for d in range(1, 8)
            ]
        )
        keep_dz.append(pltpu.make_async_copy(dz_send.at[h, :, slot], home, keep_sem.at[h, 5]))

    for copy in loads:
        copy.wait()
    for u in range(CHUNKS):
        h, e = u // 2, u % 2

        @pl.loop(0, 5)
        def _(f):
            for k in range(4):
                apart[u, k, f] = own[h, f, pl.ds(2 * k + e, ROWS, stride=PLANES), :]

        if u == 0:
            pl.semaphore_wait(barrier, 12)
        z1[u].start()
        for copy in x1[u]:
            copy.start()
        for copy in y1[u]:
            copy.start()
        keeps[u][0].start()
        keeps[u][2].start()

    load_wall.wait()

    @pl.loop(0, HALF // 64)
    def _(i):
        rows = pl.ds(i * 64, 64)
        high, low = split(wall_f[rows, :])
        wall_h[rows, :] = high
        wall_l[rows, :] = low

    high, low = [
        dot(order_out[z_hi], dot(part, order_in[...]).astype(jnp.bfloat16)).astype(jnp.bfloat16) for part in split(span[...])
    ]
    span_3[:, 0:NZ] = high
    span_3[:, NZ : 2 * NZ] = high
    span_3[:, 2 * NZ : 3 * NZ] = low
    for u in range(CHUNKS):
        for f in range(5):
            lines_y[u, f, 0:PAD, :] = jnp.zeros((PAD, LANES), jnp.float32)
            lines_y[u, f, PAD + NY : 2 * PAD + NY, :] = jnp.zeros((PAD, LANES), jnp.float32)

    @pl.loop(0, ROWS * PLANES // 64)
    def _(i):
        rows = pl.ds(i * 64, 64)
        c = [jnp.concatenate([own[0, f, rows, :], own[1, f, rows, :]], axis=1) for f in range(5)]
        for f, value in enumerate(flux_along(c, 0)):
            high, low = split(value)
            along = (dot(high, shift[...]) + dot(low, shift[...])) * (1.0 / 12.0)
            value = c[f] - TIME_STEP * along
            for h in range(2):
                own[h, f, rows, :] = value[:, h * LANES : (h + 1) * LANES]

    save = pltpu.make_async_copy(own, base_out, load_sem.at[0])
    save.start()

    def pass_near(u):
        z1[u].wait_recv()
        z2[u].start()
        for copy in x2[u]:
            copy.start()
        keeps[u][1].start()

    def pass_far(u):
        z2[u].wait_recv()
        for copy in y2[u]:
            copy.start()
        keeps[u][3].start()

    def derive_y(u):
        keeps[u][0].wait()
        keeps[u][1].wait()
        for copy in x1[u] + x2[u]:
            copy.wait_recv()

        @pl.loop(0, NY // 64)
        def _(i):
            r = pl.multiple_of(i * 64, 64)
            c = [lines_y[u, f, pl.ds(PAD + r, 64), :] for f in range(5)]
            for f, value in enumerate(flux_along(c, 1)):
                high, low = split(value)
                flux_h[pl.ds(r, 64), f * LANES : (f + 1) * LANES] = high
                flux_l[pl.ds(r, 64), f * LANES : (f + 1) * LANES] = low

        @pl.loop(0, 4)
        def _(k):
            rows = pl.ds(pl.multiple_of(k * ROWS, ROWS), ROWS)
            total = dot(wall_h[rows, :], flux_h[...])
            total += dot(wall_h[rows, :], flux_l[...])
            total += dot(wall_l[rows, :], flux_h[...])
            block = z_lo * 4 + k
            weight = jnp.broadcast_to(damp_rows[pl.ds(block, 1), :], (ROWS, LANES)).T
            for f in range(5):
                window = lines_y[u, f, pl.ds(pl.multiple_of(block * ROWS, ROWS), ROWS + 2 * PAD), :]

                def at(step, window=window):
                    return window[PAD + step : PAD + step + ROWS]

                smooth = at(-2) - 4.0 * at(-1) + 6.0 * at(0) - 4.0 * at(1) + at(2)
                dy_send[u, k, f] = total[:, f * LANES : (f + 1) * LANES] + weight * smooth

        for copy in x3[u]:
            copy.start()
        keeps[u][4].start()

    def derive_z(h):
        for u in (2 * h, 2 * h + 1):
            keeps[u][2].wait()
            keeps[u][3].wait()
            for copy in y1[u] + y2[u]:
                copy.wait_recv()
        lines = lines_z.reshape(CHUNKS, GZ * 4 * 5 * HOLD, LANES)
        results = dz_send.reshape(2, 2 * 8 * 4 * 5 * HOLD, LANES)

        @pl.loop(0, HOLD)
        def _(r):
            weight = damp[gy * ROWS + slot * HOLD + r]
            c = []
            for f in range(5):
                at = pl.ds(f * HOLD + r, NZ // 2, stride=5 * HOLD)
                c.append(jnp.concatenate([lines[2 * h, at, :], lines[2 * h + 1, at, :]], axis=0))
            high, low = split(jnp.concatenate(flux_along(c, 2), axis=1))
            total = dot(span_3[...], jnp.concatenate([high, low, high], axis=0))
            high, low = split(jnp.concatenate(c, axis=1))
            total += weight * dot(fourth[z_hi], jnp.concatenate([high, low], axis=0))
            for f in range(5):
                at = pl.ds(f * HOLD + r, NZ // 2, stride=5 * HOLD)
                results[h, at, :] = total[:, f * LANES : (f + 1) * LANES]

        for copy in y3[h]:
            copy.start()
        keep_dz[h].start()

    pass_near(0)
    pass_near(1)
    pass_far(0)
    derive_y(0)
    pass_near(2)
    pass_far(1)
    derive_y(1)
    derive_z(0)
    pass_near(3)
    pass_far(2)
    derive_y(2)
    pass_far(3)
    derive_y(3)
    derive_z(1)

    save.wait()
    for u in range(CHUNKS):
        z1[u].wait_send()
        z2[u].wait_send()
        keeps[u][4].wait()
        for copy in x1[u] + x2[u] + y1[u] + y2[u]:
            copy.wait_send()
        for copy in x3[u]:
            copy.wait()
    for h in range(2):
        keep_dz[h].wait()
        for copy in y3[h]:
            copy.wait()


def finish(base, dy, dz, new_dens, new_mom, new_ene, turned):
    count = new_dens.shape[0] // PLANES
    for f in range(5):
        halves = []
        for h in range(2):
            for e in range(2):
                for k in range(4):
                    u = 2 * h + e
                    turned[h, f, pl.ds(2 * k + e, count, stride=PLANES), :] = dy[u, k, f] + dz[u, k, f]
            halves.append(base[h, f] - TIME_STEP * turned[h, f])
        value = jnp.concatenate(halves, axis=1)
        if f == 0:
            new_dens[...] = value
        elif f == 4:
            new_ene[...] = value
        else:
            new_mom[f - 1] = value


def plane_order():
    return np.arange(NZ).reshape(GZ, 4, 2).transpose(2, 0, 1).reshape(-1)


def half_order(z_hi):
    return np.arange(NZ).reshape(4, 2, 2, 4, 2)[:, z_hi].transpose(3, 0, 1, 2).reshape(-1)


def order_matrices():
    eye = np.eye(NZ, dtype=np.float32)
    return eye[:, plane_order()], np.stack([eye[half_order(z)] for z in range(2)])


def fourth_matrix():
    m = np.zeros((NZ, NZ), np.float32)
    for i in range(NZ):
        for k, w in ((-2, 1.0), (-1, -4.0), (0, 6.0), (1, -4.0), (2, 1.0)):
            m[i, (i + k) % NZ] += w
    m = np.stack([m[half_order(z)][:, plane_order()] for z in range(2)])
    return np.concatenate([m, m], axis=2)


def shift_matrix():
    m = np.zeros((CELLS, CELLS), np.float32)
    for i in range(CELLS):
        for k, w in ((1, 8.0), (-1, -8.0), (2, -1.0), (-2, 1.0)):
            m[min(max(i + k, 0), CELLS - 1), i] += w
    return m


ANY = pl.BlockSpec(memory_space=pl.ANY)
VMEM = pl.BlockSpec(memory_space=pltpu.VMEM)
SMEM = pl.BlockSpec(memory_space=pltpu.SMEM)
DMA = pltpu.SemaphoreType.DMA


def local(density, momentum, energy, wall_operator, span_operator, damping):
    cells = ROWS * PLANES
    dens = density.reshape(cells, CELLS)
    mom = momentum.reshape(3, cells, CELLS)
    ene = energy.reshape(cells, CELLS)
    f32, bf16 = jnp.float32, jnp.bfloat16
    order_in, order_out = order_matrices()
    whole = jax.ShapeDtypeStruct((CHUNKS, 4, 5, ROWS, LANES), f32)
    dy, dz, base, _, _ = pl.pallas_call(
        exchange,
        out_shape=(whole, whole, jax.ShapeDtypeStruct((2, 5, cells, LANES), f32), whole, whole),
        in_specs=[ANY, ANY, ANY, ANY, VMEM, SMEM, VMEM, VMEM, VMEM, VMEM, VMEM],
        out_specs=(ANY,) * 5,
        scratch_shapes=[
            pltpu.VMEM((2, 5, cells, LANES), f32),
            pltpu.VMEM((CHUNKS, 4, 5, ROWS, LANES), f32),
            pltpu.VMEM((CHUNKS, 5, NY + 2 * PAD, LANES), f32),
            pltpu.VMEM((CHUNKS, GZ, 4, 5, HOLD, LANES), f32),
            pltpu.VMEM((CHUNKS, 4, 5, ROWS, LANES), f32),
            pltpu.VMEM((2, 2, 8, 4, 5, HOLD, LANES), f32),
            pltpu.VMEM((HALF, NY), f32),
            pltpu.VMEM((HALF, NY), bf16),
            pltpu.VMEM((HALF, NY), bf16),
            pltpu.VMEM((NY, 5 * LANES), bf16),
            pltpu.VMEM((NY, 5 * LANES), bf16),
            pltpu.VMEM((NZ // 2, 3 * NZ), bf16),
            *[DMA((CHUNKS,))] * 4,
            *[DMA((CHUNKS, 3))] * 6,
            *[DMA((CHUNKS, 7))] * 4,
            *[DMA((2, 7))] * 2,
            DMA((7,)),
            DMA((CHUNKS, 6)),
        ],
        compiler_params=pltpu.CompilerParams(
            collective_id=0, has_side_effects=True, vmem_limit_bytes=62 << 20
        ),
        name="exchange",
    )(
        dens, mom, ene, wall_operator, span_operator, damping, damping.reshape(GY, ROWS),
        jnp.asarray(fourth_matrix(), bf16), jnp.asarray(order_in, bf16), jnp.asarray(order_out, bf16),
        jnp.asarray(shift_matrix(), bf16),
    )
    steps = 16
    block = cells // steps
    field = pl.BlockSpec((block, CELLS), lambda i: (i, 0))
    three = pl.BlockSpec((3, block, CELLS), lambda i: (0, i, 0))
    apart = pl.BlockSpec((CHUNKS, 4, 5, ROWS // steps, LANES), lambda i: (0, 0, 0, i, 0))
    new = pl.pallas_call(
        finish,
        grid=(steps,),
        out_shape=(
            jax.ShapeDtypeStruct((cells, CELLS), f32),
            jax.ShapeDtypeStruct((3, cells, CELLS), f32),
            jax.ShapeDtypeStruct((cells, CELLS), f32),
        ),
        in_specs=[pl.BlockSpec((2, 5, block, LANES), lambda i: (0, 0, i, 0)), apart, apart],
        out_specs=(field, three, field),
        scratch_shapes=[pltpu.VMEM((2, 5, block, LANES), f32)],
        name="finish",
    )(base, dy, dz)
    shape = (ROWS, PLANES, CELLS)
    return new[0].reshape(shape), new[1].reshape((3,) + shape), new[2].reshape(shape)


def solution(mesh):
    in_specs = (P("gy", "gz", None), P(None, "gy", "gz", None), P("gy", "gz", None), P(), P(), P())
    out_specs = (P("gy", "gz", None), P(None, "gy", "gz", None), P("gy", "gz", None))
    return jax.shard_map(local, mesh=mesh, in_specs=in_specs, out_specs=out_specs, check_vma=False)
```

time: 263 us -> 228 us (0.87); the launches traced: 259 us -> 227 us
  Pallas kernels: 257 us -> 227 us
    pallas_call x1, Pallas kernels: 242 us -> 214 us  [local(): pl.pallas_call(exchange, out_shape=(whole, whole, jax.ShapeDtypeStruct((2...]
where the time goes in v2:
time: 228 us; the launch traced here: 227 us
  Pallas kernels  227 us (100%)
    pallas_call x1, Pallas kernels, local(): pl.pallas_call(exchange, out_shape=(whole, whole, jax.ShapeDtypeStruct((2...  214 us
    pallas_call x1, Pallas kernels, local(): pl.pallas_call(finish, grid=(steps,), out_shape=(jax.ShapeDtypeStruct((ce...  13 us

profile of v2, /device:TPU:1, one launch (start us, length us, event | category | flops | bytes accessed | tf_op | source)
XLA Modules:
  0.0 227.3 jit_solution(10653572160740100779)
XLA Ops:
  0.6 213.7 %exchange.1 = (f32[4,4,5,128,128]{4,3,2,1,0:T(8,128)}, f32[4,4,5,128,128]{4,3,2,1,0:T(8,128)}, f32[2,5,1024,128]{3,2,1,0:T(8,128)}, f32[4,4,5,128,128]{4,3,2,1,0:T(8,128)}, f32[4,4,5,128,128]{4,3,2,1,0:T(8,128)}) custom-call(f32[1024,256]{1,0:T(8,128)} %bitcast.8, f32[3,1024,256]{2,1,0:T(8,128)} %bitcast.7, f32[1024,256]{1,0:T(8,128)} %bitcast.9, ...), custom_call_target="tpu_custom_call" | custom-call | tf_op jit(solution)/shard_map/exchange/pallas_call | solution.py:366
  214.3 13.0 %finish.1 = (f32[1024,256]{1,0:T(8,128)}, f32[3,1024,256]{2,1,0:T(8,128)}, f32[1024,256]{1,0:T(8,128)}) custom-call(f32[2,5,1024,128]{3,2,1,0:T(8,128)} %get-tuple-element.9.base, f32[4,4,5,128,128]{4,3,2,1,0:T(8,128)} %get-tuple-element.10.dy, f32[4,4,5,128,128]{4,3,2,1,0:T(8,128)} %get-tuple-element.11.dz), custom_call_target="tpu_custom_call" | custom-call | tf_op jit(solution)/shard_map/finish/pallas_call | solution.py:405

commit v3 on v2

--- a/solution.py
+++ b/solution.py
@@ -47,8 +47,8 @@
 
 def exchange(
     dens, mom, ene, wall, span, damp, damp_rows, fourth, order_in, order_out, shift,
-    dy_out, dz_out, base_out, near, far,
-    own, apart, lines_y, lines_z, dy_send, dz_send, wall_f, wall_h, wall_l, flux_h, flux_l, span_3,
+    new_out, near, far,
+    dy_out, dz_out, own, apart, lines_y, lines_z, dy_send, dz_send, wall_f, wall_h, wall_l, flux_h, flux_l, span_3,
     z1s, z1r, z2s, z2r, x1s, x1r, x2s, x2r, x3s, x3r, y1s, y1r, y2s, y2r, y3s, y3r, load_sem, keep_sem,
 ):
     gy = lax.axis_index("gy")
@@ -86,8 +86,18 @@
     for peer in [pair, relay] + x_peers[1:] + y_peers[1:]:
         pl.semaphore_signal(barrier, inc=1, device_id=peer, device_id_type=MESH)
 
-    z1 = [send(apart.at[u], near.at[u], z1s.at[u], z1r.at[u], pair) for u in range(CHUNKS)]
-    z2 = [send(near.at[u], far.at[u], z2s.at[u], z2r.at[u], relay) for u in range(CHUNKS)]
+    z1, z2 = [], []
+    for u in range(CHUNKS):
+        for copies, source, target, ssem, rsem, peer in (
+            (z1, apart, near, z1s, z1r, pair),
+            (z2, near, far, z2s, z2r, relay),
+        ):
+            copies.append(
+                [
+                    send(source.at[u, pl.ds(2 * j, 2)], target.at[u, pl.ds(2 * j, 2)], ssem.at[u, j], rsem.at[u, j], peer)
+                    for j in range(2)
+                ]
+            )
     x1, x2, x3, keeps = [], [], [], []
     for u in range(CHUNKS):
         for copies, source, row, ssem, rsem in ((x1, apart, near_row, x1s, x1r), (x2, near, far_row, x2s, x2r)):
@@ -119,16 +129,28 @@
         )
     y1, y2, y3, keep_dz = [], [], [], []
     for u in range(CHUNKS):
-        for copies, source, index, ssem, rsem in ((y1, apart, gz, y1s, y1r), (y2, far, far_gz, y2s, y2r)):
-            copies.append(
+        y1.append(
+            [
+                send(
+                    apart.at[u, :, :, pl.ds(slot_of[d] * HOLD, HOLD), :], lines_z.at[u, gz],
+                    y1s.at[u, d - 1], y1r.at[u, d - 1], y_peers[d],
+                )
+                for d in range(1, 8)
+            ]
+        )
+        y2.append(
+            [
                 [
                     send(
-                        source.at[u, :, :, pl.ds(slot_of[d] * HOLD, HOLD), :], lines_z.at[u, index],
-                        ssem.at[u, d - 1], rsem.at[u, d - 1], y_peers[d],
+                        far.at[u, pl.ds(2 * j, 2), :, pl.ds(slot_of[d] * HOLD, HOLD), :],
+                        lines_z.at[u, far_gz, pl.ds(2 * j, 2)],
+                        y2s.at[u, j, d - 1], y2r.at[u, j, d - 1], y_peers[d],
                     )
                     for d in range(1, 8)
                 ]
-            )
+                for j in range(2)
+            ]
+        )
     for h in range(2):
         home = dz_out.at[pl.ds(2 * h, 2), :, :, pl.ds(slot * HOLD, HOLD), :]
         y3.append(
@@ -151,7 +173,8 @@
 
         if u == 0:
             pl.semaphore_wait(barrier, 12)
-        z1[u].start()
+        for copy in z1[u]:
+            copy.start()
         for copy in x1[u]:
             copy.start()
         for copy in y1[u]:
@@ -190,21 +213,20 @@
             for h in range(2):
                 own[h, f, rows, :] = value[:, h * LANES : (h + 1) * LANES]
 
-    save = pltpu.make_async_copy(own, base_out, load_sem.at[0])
-    save.start()
-
-    def pass_near(u):
-        z1[u].wait_recv()
-        z2[u].start()
-        for copy in x2[u]:
-            copy.start()
-        keeps[u][1].start()
-
-    def pass_far(u):
-        z2[u].wait_recv()
-        for copy in y2[u]:
-            copy.start()
-        keeps[u][3].start()
+    def pass_near(u, j):
+        z1[u][j].wait_recv()
+        z2[u][j].start()
+        if j == 1:
+            for copy in x2[u]:
+                copy.start()
+            keeps[u][1].start()
+
+    def pass_far(u, j):
+        z2[u][j].wait_recv()
+        for copy in y2[u][j]:
+            copy.start()
+        if j == 1:
+            keeps[u][3].start()
 
     def derive_y(u):
         keeps[u][0].wait()
@@ -246,7 +268,7 @@
         for u in (2 * h, 2 * h + 1):
             keeps[u][2].wait()
             keeps[u][3].wait()
-            for copy in y1[u] + y2[u]:
+            for copy in y1[u] + y2[u][0] + y2[u][1]:
                 copy.wait_recv()
         lines = lines_z.reshape(CHUNKS, GZ * 4 * 5 * HOLD, LANES)
         results = dz_send.reshape(2, 2 * 8 * 4 * 5 * HOLD, LANES)
@@ -270,53 +292,85 @@
             copy.start()
         keep_dz[h].start()
 
-    pass_near(0)
-    pass_near(1)
-    pass_far(0)
-    derive_y(0)
-    pass_near(2)
-    pass_far(1)
-    derive_y(1)
-    derive_z(0)
-    pass_near(3)
-    pass_far(2)
-    derive_y(2)
-    pass_far(3)
-    derive_y(3)
-    derive_z(1)
-
-    save.wait()
-    for u in range(CHUNKS):
-        z1[u].wait_send()
-        z2[u].wait_send()
-        keeps[u][4].wait()
-        for copy in x1[u] + x2[u] + y1[u] + y2[u]:
-            copy.wait_send()
-        for copy in x3[u]:
-            copy.wait()
-    for h in range(2):
+    def add(h, source):
+        @pl.loop(0, 5)
+        def _(f):
+            for e in range(2):
+                for k in range(4):
+                    at = pl.ds(2 * k + e, ROWS, stride=PLANES)
+                    own[h, f, at, :] = own[h, f, at, :] - TIME_STEP * source[2 * h + e, k, f]
+
+    def add_y(h):
+        for u in (2 * h, 2 * h + 1):
+            keeps[u][4].wait()
+            for copy in x3[u]:
+                copy.wait_recv()
+        add(h, dy_out)
+
+    saves = [pltpu.make_async_copy(own.at[h], new_out.at[h], load_sem.at[h]) for h in range(2)]
+
+    def add_z(h):
         keep_dz[h].wait()
         for copy in y3[h]:
+            copy.wait_recv()
+        add(h, dz_out)
+        saves[h].start()
+
+    pass_near(0, 0)
+    pass_near(0, 1)
+    pass_far(0, 0)
+    pass_near(1, 0)
+    pass_far(0, 1)
+    pass_near(1, 1)
+    pass_far(1, 0)
+    pass_near(2, 0)
+    pass_far(1, 1)
+    derive_y(0)
+    pass_near(2, 1)
+    pass_far(2, 0)
+    derive_z(0)
+    derive_y(1)
+    pass_near(3, 0)
+    pass_far(2, 1)
+    pass_near(3, 1)
+    pass_far(3, 0)
+    derive_y(2)
+    pass_far(3, 1)
+    derive_z(1)
+    derive_y(3)
+    add_y(0)
+    add_z(0)
+    add_y(1)
+    add_z(1)
+
+    for h in range(2):
+        saves[h].wait()
+        for copy in y3[h]:
+            copy.wait_send()
+    for u in range(CHUNKS):
+        for copy in z1[u] + z2[u] + x1[u] + x2[u] + x3[u] + y1[u] + y2[u][0] + y2[u][1]:
+            copy.wait_send()
+
+
+def join(halves, new_dens, new_mom, new_ene, whole, in_sem, out_sem):
+    targets = [new_dens, new_mom.at[0], new_mom.at[1], new_mom.at[2], new_ene]
+    ins = [
+        [
+            pltpu.make_async_copy(halves.at[h, f], whole.at[f, :, pl.ds(h * LANES, LANES)], in_sem.at[f, h])
+            for h in range(2)
+        ]
+        for f in range(5)
+    ]
+    outs = [pltpu.make_async_copy(whole.at[f], targets[f], out_sem.at[f]) for f in range(5)]
+    for f in range(5):
+        for copy in ins[f]:
+            copy.start()
+    for f in range(5):
+        for copy in ins[f]:
             copy.wait()
-
-
-def finish(base, dy, dz, new_dens, new_mom, new_ene, turned):
-    count = new_dens.shape[0] // PLANES
-    for f in range(5):
-        halves = []
-        for h in range(2):
-            for e in range(2):
-                for k in range(4):
-                    u = 2 * h + e
-                    turned[h, f, pl.ds(2 * k + e, count, stride=PLANES), :] = dy[u, k, f] + dz[u, k, f]
-            halves.append(base[h, f] - TIME_STEP * turned[h, f])
-        value = jnp.concatenate(halves, axis=1)
-        if f == 0:
-            new_dens[...] = value
-        elif f == 4:
-            new_ene[...] = value
-        else:
-            new_mom[f - 1] = value
+        outs[f].start()
+    for copy in outs:
+        copy.wait()
 
 
 def plane_order():
@@ -363,12 +417,14 @@
     f32, bf16 = jnp.float32, jnp.bfloat16
     order_in, order_out = order_matrices()
     whole = jax.ShapeDtypeStruct((CHUNKS, 4, 5, ROWS, LANES), f32)
-    dy, dz, base, _, _ = pl.pallas_call(
+    halves, _, _ = pl.pallas_call(
         exchange,
-        out_shape=(whole, whole, jax.ShapeDtypeStruct((2, 5, cells, LANES), f32), whole, whole),
+        out_shape=(jax.ShapeDtypeStruct((2, 5, cells, LANES), f32), whole, whole),
         in_specs=[ANY, ANY, ANY, ANY, VMEM, SMEM, VMEM, VMEM, VMEM, VMEM, VMEM],
-        out_specs=(ANY,) * 5,
+        out_specs=(ANY,) * 3,
         scratch_shapes=[
+            pltpu.VMEM((CHUNKS, 4, 5, ROWS, LANES), f32),
+            pltpu.VMEM((CHUNKS, 4, 5, ROWS, LANES), f32),
             pltpu.VMEM((2, 5, cells, LANES), f32),
             pltpu.VMEM((CHUNKS, 4, 5, ROWS, LANES), f32),
             pltpu.VMEM((CHUNKS, 5, NY + 2 * PAD, LANES), f32),
@@ -381,9 +437,10 @@
             pltpu.VMEM((NY, 5 * LANES), bf16),
             pltpu.VMEM((NY, 5 * LANES), bf16),
             pltpu.VMEM((NZ // 2, 3 * NZ), bf16),
-            *[DMA((CHUNKS,))] * 4,
+            *[DMA((CHUNKS, 2))] * 4,
             *[DMA((CHUNKS, 3))] * 6,
-            *[DMA((CHUNKS, 7))] * 4,
+            *[DMA((CHUNKS, 7))] * 2,
+            *[DMA((CHUNKS, 2, 7))] * 2,
             *[DMA((2, 7))] * 2,
             DMA((7,)),
             DMA((CHUNKS, 6)),
@@ -397,24 +454,18 @@
         jnp.asarray(fourth_matrix(), bf16), jnp.asarray(order_in, bf16), jnp.asarray(order_out, bf16),
         jnp.asarray(shift_matrix(), bf16),
     )
-    steps = 16
-    block = cells // steps
-    field = pl.BlockSpec((block, CELLS), lambda i: (i, 0))
-    three = pl.BlockSpec((3, block, CELLS), lambda i: (0, i, 0))
-    apart = pl.BlockSpec((CHUNKS, 4, 5, ROWS // steps, LANES), lambda i: (0, 0, 0, i, 0))
     new = pl.pallas_call(
-        finish,
-        grid=(steps,),
+        join,
         out_shape=(
             jax.ShapeDtypeStruct((cells, CELLS), f32),
             jax.ShapeDtypeStruct((3, cells, CELLS), f32),
             jax.ShapeDtypeStruct((cells, CELLS), f32),
         ),
-        in_specs=[pl.BlockSpec((2, 5, block, LANES), lambda i: (0, 0, i, 0)), apart, apart],
-        out_specs=(field, three, field),
-        scratch_shapes=[pltpu.VMEM((2, 5, block, LANES), f32)],
-        name="finish",
-    )(base, dy, dz)
+        in_specs=[ANY],
+        out_specs=(ANY,) * 3,
+        scratch_shapes=[pltpu.VMEM((5, cells, CELLS), f32), DMA((5, 2)), DMA((5,))],
+        name="join",
+    )(halves)
     shape = (ROWS, PLANES, CELLS)
     return new[0].reshape(shape), new[1].reshape((3,) + shape), new[2].reshape(shape)
 

time: 228 us -> 202 us (0.89)
  Pallas kernels: 227 us -> 201 us
    pallas_call x2, Pallas kernels: 227 us -> 201 us  [the longest x1 197 us: local(): pl.pallas_call(exchange, out_shape=(jax.ShapeDtypeStruct((2, 5, cells, LA...]
where the time goes in v3:
time: 202 us
  Pallas kernels  201 us (100%)
    pallas_call x1, Pallas kernels, local(): pl.pallas_call(exchange, out_shape=(jax.ShapeDtypeStruct((2, 5, cells, LA...  197 us
    pallas_call x1, Pallas kernels, local(): pl.pallas_call(join, out_shape=(jax.ShapeDtypeStruct((cells, CELLS), f32)...  4.46 us

profile of v3, /device:TPU:1, one launch (start us, length us, event | category | flops | bytes accessed | tf_op | source)
XLA Modules:
  0.0 202.0 jit_solution(1672374995383277837)
XLA Ops:
  0.6 196.9 %exchange.1 = (f32[2,5,1024,128]{3,2,1,0:T(8,128)}, f32[4,4,5,128,128]{4,3,2,1,0:T(8,128)}, f32[4,4,5,128,128]{4,3,2,1,0:T(8,128)}) custom-call(f32[1024,256]{1,0:T(8,128)} %bitcast.8, f32[3,1024,256]{2,1,0:T(8,128)} %bitcast.7, f32[1024,256]{1,0:T(8,128)} %bitcast.9, f32[1024,1024]{1,0:T(8,128)} %wall.1, f32[128,128]{1,0:T(8,128)} %span.1, f32[1024]{0:T(1024)} %damp.1, ...), custom_call_target="tpu_custom_call" | custom-call | tf_op jit(solution)/shard_map/exchange/pallas_call | solution.py:420
  197.6 4.5 %join.1 = (f32[1024,256]{1,0:T(8,128)}, f32[3,1024,256]{2,1,0:T(8,128)}, f32[1024,256]{1,0:T(8,128)}) custom-call(f32[2,5,1024,128]{3,2,1,0:T(8,128)} %get-tuple-element.7.halves), custom_call_target="tpu_custom_call" | custom-call | tf_op jit(solution)/shard_map/join/pallas_call | solution.py:457

commit v4 on v3

--- a/solution.py
+++ b/solution.py
@@ -17,7 +17,7 @@
 HOLD = 16
 CHUNKS = 4
 HALF = NY // 2
-PAD = 8
+GROUPS = ROWS // HOLD
 
 
 def flux_along(c, direction):
@@ -48,8 +48,8 @@
 def exchange(
     dens, mom, ene, wall, span, damp, damp_rows, fourth, order_in, order_out, shift,
     new_out, near, far,
-    dy_out, dz_out, own, apart, lines_y, lines_z, dy_send, dz_send, wall_f, wall_h, wall_l, flux_h, flux_l, span_3,
-    z1s, z1r, z2s, z2r, x1s, x1r, x2s, x2r, x3s, x3r, y1s, y1r, y2s, y2r, y3s, y3r, load_sem, keep_sem,
+    dy_out, dz_out, own, apart, lines_y, lines_z, dy_send, dz_send, wall_f, wall_h, wall_l, flux_h, flux_l, span_2,
+    z1s, z1r, z2s, z2r, x1s, x1r, x2s, x2r, x3s, x3r, y1s, y1r, y2s, y2r, y3s, y3r, load_sem, keep_sem, save_sem,
 ):
     gy = lax.axis_index("gy")
     gz = lax.axis_index("gz")
@@ -63,8 +63,8 @@
     slot_of = [lax.rem(slot + d, 8) for d in range(8)]
     y_peers = [(gy, (other // 2) * 4 + z_hi * 2 + lax.rem(other, 2)) for other in slot_of]
     far_gz = y * 4 + (1 - z_hi) * 2 + core
-    near_row = PAD + gy * ROWS
-    far_row = PAD + pair[0] * ROWS
+    near_group = 1 + gy * GROUPS
+    far_group = 1 + pair[0] * GROUPS
 
     def send(src, dst, ssem, rsem, peer):
         return pltpu.make_async_remote_copy(src, dst, ssem, rsem, device_id=peer, device_id_type=MESH)
@@ -80,7 +80,6 @@
     load_wall = pltpu.make_async_copy(wall.at[pl.ds(z_lo * HALF, HALF), :], wall_f, load_sem.at[6])
     for copy in loads:
         copy.start()
-    load_wall.start()
 
     barrier = pltpu.get_barrier_semaphore()
     for peer in [pair, relay] + x_peers[1:] + y_peers[1:]:
@@ -94,17 +93,17 @@
         ):
             copies.append(
                 [
-                    send(source.at[u, pl.ds(2 * j, 2)], target.at[u, pl.ds(2 * j, 2)], ssem.at[u, j], rsem.at[u, j], peer)
+                    send(source.at[u, :, pl.ds(2 * j, 2)], target.at[u, :, pl.ds(2 * j, 2)], ssem.at[u, j], rsem.at[u, j], peer)
                     for j in range(2)
                 ]
             )
     x1, x2, x3, keeps = [], [], [], []
     for u in range(CHUNKS):
-        for copies, source, row, ssem, rsem in ((x1, apart, near_row, x1s, x1r), (x2, near, far_row, x2s, x2r)):
-            target = lines_y.at[u, :, pl.ds(row, ROWS), :]
+        for copies, source, group, ssem, rsem in ((x1, apart, near_group, x1s, x1r), (x2, near, far_group, x2s, x2r)):
+            target = lines_y.at[u, pl.ds(group, GROUPS)]
             copies.append(
                 [
-                    send(source.at[u, x_of[d]], target, ssem.at[u, d - 1], rsem.at[u, d - 1], x_peers[d])
+                    send(source.at[u, :, x_of[d]], target, ssem.at[u, d - 1], rsem.at[u, d - 1], x_peers[d])
                     for d in range(1, 4)
                 ]
             )
@@ -116,13 +115,13 @@
         )
         keeps.append(
             [
-                pltpu.make_async_copy(apart.at[u, x], lines_y.at[u, :, pl.ds(near_row, ROWS), :], keep_sem.at[u, 0]),
-                pltpu.make_async_copy(near.at[u, x], lines_y.at[u, :, pl.ds(far_row, ROWS), :], keep_sem.at[u, 1]),
+                pltpu.make_async_copy(apart.at[u, :, x], lines_y.at[u, pl.ds(near_group, GROUPS)], keep_sem.at[u, 0]),
+                pltpu.make_async_copy(near.at[u, :, x], lines_y.at[u, pl.ds(far_group, GROUPS)], keep_sem.at[u, 1]),
                 pltpu.make_async_copy(
-                    apart.at[u, :, :, pl.ds(slot * HOLD, HOLD), :], lines_z.at[u, gz], keep_sem.at[u, 2]
+                    apart.at[u, slot], lines_z.at[u, gz], keep_sem.at[u, 2]
                 ),
                 pltpu.make_async_copy(
-                    far.at[u, :, :, pl.ds(slot * HOLD, HOLD), :], lines_z.at[u, far_gz], keep_sem.at[u, 3]
+                    far.at[u, slot], lines_z.at[u, far_gz], keep_sem.at[u, 3]
                 ),
                 pltpu.make_async_copy(dy_send.at[u, x], dy_out.at[u, x], keep_sem.at[u, 4]),
             ]
@@ -132,7 +131,7 @@
         y1.append(
             [
                 send(
-                    apart.at[u, :, :, pl.ds(slot_of[d] * HOLD, HOLD), :], lines_z.at[u, gz],
+                    apart.at[u, slot_of[d]], lines_z.at[u, gz],
                     y1s.at[u, d - 1], y1r.at[u, d - 1], y_peers[d],
                 )
                 for d in range(1, 8)
@@ -142,7 +141,7 @@
             [
                 [
                     send(
-                        far.at[u, pl.ds(2 * j, 2), :, pl.ds(slot_of[d] * HOLD, HOLD), :],
+                        far.at[u, slot_of[d], pl.ds(2 * j, 2)],
                         lines_z.at[u, far_gz, pl.ds(2 * j, 2)],
                         y2s.at[u, j, d - 1], y2r.at[u, j, d - 1], y_peers[d],
                     )
@@ -152,24 +151,33 @@
             ]
         )
     for h in range(2):
-        home = dz_out.at[pl.ds(2 * h, 2), :, :, pl.ds(slot * HOLD, HOLD), :]
+        home = dz_out.at[pl.ds(2 * h, 2), slot]
         y3.append(
             [
-                send(dz_send.at[h, :, slot_of[d]], home, y3s.at[h, d - 1], y3r.at[h, d - 1], y_peers[d])
-                for d in range(1, 8)
+                [
+                    send(
+                        dz_send.at[h, :, slot_of[d], :, :, pl.ds(8 * part, 8), :],
+                        dz_out.at[pl.ds(2 * h, 2), slot, :, :, pl.ds(8 * part, 8), :],
+                        y3s.at[h, part, d - 1], y3r.at[h, part, d - 1], y_peers[d],
+                    )
+                    for d in range(1, 8)
+                ]
+                for part in range(2)
             ]
         )
         keep_dz.append(pltpu.make_async_copy(dz_send.at[h, :, slot], home, keep_sem.at[h, 5]))
 
-    for copy in loads:
-        copy.wait()
     for u in range(CHUNKS):
         h, e = u // 2, u % 2
+        if e == 0:
+            for copy in loads[3 * h : 3 * h + 3]:
+                copy.wait()
 
         @pl.loop(0, 5)
         def _(f):
             for k in range(4):
-                apart[u, k, f] = own[h, f, pl.ds(2 * k + e, ROWS, stride=PLANES), :]
+                planes = own[h, f, pl.ds(2 * k + e, ROWS, stride=PLANES), :]
+                apart[u, :, k, f] = planes.reshape(GROUPS, HOLD, LANES)
 
         if u == 0:
             pl.semaphore_wait(barrier, 12)
@@ -181,6 +189,8 @@
             copy.start()
         keeps[u][0].start()
         keeps[u][2].start()
+
+    load_wall.start()
 
     load_wall.wait()
 
@@ -194,13 +204,14 @@
     high, low = [
         dot(order_out[z_hi], dot(part, order_in[...]).astype(jnp.bfloat16)).astype(jnp.bfloat16) for part in split(span[...])
     ]
-    span_3[:, 0:NZ] = high
-    span_3[:, NZ : 2 * NZ] = high
-    span_3[:, 2 * NZ : 3 * NZ] = low
+    span_2[0 : NZ // 2, 0:NZ] = high
+    span_2[0 : NZ // 2, NZ : 2 * NZ] = high
+    span_2[NZ // 2 : NZ, 0:NZ] = low
+    span_2[NZ // 2 : NZ, NZ : 2 * NZ] = jnp.zeros((NZ // 2, NZ), jnp.bfloat16)
     for u in range(CHUNKS):
         for f in range(5):
-            lines_y[u, f, 0:PAD, :] = jnp.zeros((PAD, LANES), jnp.float32)
-            lines_y[u, f, PAD + NY : 2 * PAD + NY, :] = jnp.zeros((PAD, LANES), jnp.float32)
+            for group in (0, NY // HOLD + 1):
+                lines_y[u, group, f] = jnp.zeros((HOLD, LANES), jnp.float32)
 
     @pl.loop(0, ROWS * PLANES // 64)
     def _(i):
@@ -237,7 +248,7 @@
         @pl.loop(0, NY // 64)
         def _(i):
             r = pl.multiple_of(i * 64, 64)
-            c = [lines_y[u, f, pl.ds(PAD + r, 64), :] for f in range(5)]
+            c = [lines_y[u, pl.ds(1 + i * 4, 4), f].reshape(64, LANES) for f in range(5)]
             for f, value in enumerate(flux_along(c, 1)):
                 high, low = split(value)
                 flux_h[pl.ds(r, 64), f * LANES : (f + 1) * LANES] = high
@@ -252,13 +263,14 @@
             block = z_lo * 4 + k
             weight = jnp.broadcast_to(damp_rows[pl.ds(block, 1), :], (ROWS, LANES)).T
             for f in range(5):
-                window = lines_y[u, f, pl.ds(pl.multiple_of(block * ROWS, ROWS), ROWS + 2 * PAD), :]
+                window = lines_y[u, pl.ds(block * GROUPS, GROUPS + 2), f].reshape(ROWS + 2 * HOLD, LANES)
 
                 def at(step, window=window):
-                    return window[PAD + step : PAD + step + ROWS]
+                    return window[HOLD + step : HOLD + step + ROWS]
 
                 smooth = at(-2) - 4.0 * at(-1) + 6.0 * at(0) - 4.0 * at(1) + at(2)
-                dy_send[u, k, f] = total[:, f * LANES : (f + 1) * LANES] + weight * smooth
+                total_f = total[:, f * LANES : (f + 1) * LANES] + weight * smooth
+                dy_send[u, k, :, f] = total_f.reshape(GROUPS, HOLD, LANES)
 
         for copy in x3[u]:
             copy.start()
@@ -273,48 +285,56 @@
         lines = lines_z.reshape(CHUNKS, GZ * 4 * 5 * HOLD, LANES)
         results = dz_send.reshape(2, 2 * 8 * 4 * 5 * HOLD, LANES)
 
-        @pl.loop(0, HOLD)
-        def _(r):
-            weight = damp[gy * ROWS + slot * HOLD + r]
-            c = []
-            for f in range(5):
-                at = pl.ds(f * HOLD + r, NZ // 2, stride=5 * HOLD)
-                c.append(jnp.concatenate([lines[2 * h, at, :], lines[2 * h + 1, at, :]], axis=0))
-            high, low = split(jnp.concatenate(flux_along(c, 2), axis=1))
-            total = dot(span_3[...], jnp.concatenate([high, low, high], axis=0))
-            high, low = split(jnp.concatenate(c, axis=1))
-            total += weight * dot(fourth[z_hi], jnp.concatenate([high, low], axis=0))
-            for f in range(5):
-                at = pl.ds(f * HOLD + r, NZ // 2, stride=5 * HOLD)
-                results[h, at, :] = total[:, f * LANES : (f + 1) * LANES]
-
-        for copy in y3[h]:
-            copy.start()
+        for part in range(2):
+
+            @pl.loop(8 * part, 8 * part + 8)
+            def _(r):
+                weight = damp[gy * ROWS + slot * HOLD + r]
+                c = []
+                for f in range(5):
+                    at = pl.ds(f * HOLD + r, NZ // 2, stride=5 * HOLD)
+                    c.append(jnp.concatenate([lines[2 * h, at, :], lines[2 * h + 1, at, :]], axis=0))
+                high, low = split(jnp.concatenate(flux_along(c, 2), axis=1))
+                both = dot(span_2[...], jnp.concatenate([high, low], axis=0))
+                high, low = split(jnp.concatenate(c, axis=1))
+                total = weight * dot(fourth[z_hi], jnp.concatenate([high, low], axis=0))
+                total += both[0 : NZ // 2] + both[NZ // 2 :]
+                for f in range(5):
+                    at = pl.ds(f * HOLD + r, NZ // 2, stride=5 * HOLD)
+                    results[h, at, :] = total[:, f * LANES : (f + 1) * LANES]
+
+            for copy in y3[h][part]:
+                copy.start()
         keep_dz[h].start()
 
-    def add(h, source):
-        @pl.loop(0, 5)
-        def _(f):
-            for e in range(2):
-                for k in range(4):
-                    at = pl.ds(2 * k + e, ROWS, stride=PLANES)
-                    own[h, f, at, :] = own[h, f, at, :] - TIME_STEP * source[2 * h + e, k, f]
+    def add(h, f, source):
+        for e in range(2):
+            for k in range(4):
+                at = pl.ds(2 * k + e, ROWS, stride=PLANES)
+                part = source(2 * h + e, k).reshape(ROWS, LANES)
+                own[h, f, at, :] = own[h, f, at, :] - TIME_STEP * part
 
     def add_y(h):
         for u in (2 * h, 2 * h + 1):
             keeps[u][4].wait()
             for copy in x3[u]:
                 copy.wait_recv()
-        add(h, dy_out)
-
-    saves = [pltpu.make_async_copy(own.at[h], new_out.at[h], load_sem.at[h]) for h in range(2)]
+
+        @pl.loop(0, 5)
+        def _(f):
+            add(h, f, lambda u, k: dy_out[u, k, :, f])
+
+    saves = [
+        [pltpu.make_async_copy(own.at[h, f], new_out.at[h, f], save_sem.at[h, f]) for f in range(5)] for h in range(2)
+    ]
 
     def add_z(h):
         keep_dz[h].wait()
-        for copy in y3[h]:
+        for copy in y3[h][0] + y3[h][1]:
             copy.wait_recv()
-        add(h, dz_out)
-        saves[h].start()
+        for f in range(5):
+            add(h, f, lambda u, k, f=f: dz_out[u, :, k, f])
+            saves[h][f].start()
 
     pass_near(0, 0)
     pass_near(0, 1)
@@ -344,12 +364,13 @@
     add_z(1)
 
     for h in range(2):
-        saves[h].wait()
-        for copy in y3[h]:
+        for copy in y3[h][0] + y3[h][1]:
             copy.wait_send()
     for u in range(CHUNKS):
         for copy in z1[u] + z2[u] + x1[u] + x2[u] + x3[u] + y1[u] + y2[u][0] + y2[u][1]:
             copy.wait_send()
+    for copy in saves[0] + saves[1]:
+        copy.wait()
 
 
 def join(halves, new_dens, new_mom, new_ene, whole, in_sem, out_sem):
@@ -416,34 +437,35 @@
     ene = energy.reshape(cells, CELLS)
     f32, bf16 = jnp.float32, jnp.bfloat16
     order_in, order_out = order_matrices()
-    whole = jax.ShapeDtypeStruct((CHUNKS, 4, 5, ROWS, LANES), f32)
+    whole = jax.ShapeDtypeStruct((CHUNKS, GROUPS, 4, 5, HOLD, LANES), f32)
     halves, _, _ = pl.pallas_call(
         exchange,
         out_shape=(jax.ShapeDtypeStruct((2, 5, cells, LANES), f32), whole, whole),
         in_specs=[ANY, ANY, ANY, ANY, VMEM, SMEM, VMEM, VMEM, VMEM, VMEM, VMEM],
         out_specs=(ANY,) * 3,
         scratch_shapes=[
-            pltpu.VMEM((CHUNKS, 4, 5, ROWS, LANES), f32),
-            pltpu.VMEM((CHUNKS, 4, 5, ROWS, LANES), f32),
+            pltpu.VMEM((CHUNKS, 4, GROUPS, 5, HOLD, LANES), f32),
+            pltpu.VMEM((CHUNKS, GROUPS, 4, 5, HOLD, LANES), f32),
             pltpu.VMEM((2, 5, cells, LANES), f32),
-            pltpu.VMEM((CHUNKS, 4, 5, ROWS, LANES), f32),
-            pltpu.VMEM((CHUNKS, 5, NY + 2 * PAD, LANES), f32),
+            pltpu.VMEM((CHUNKS, GROUPS, 4, 5, HOLD, LANES), f32),
+            pltpu.VMEM((CHUNKS, NY // HOLD + 2, 5, HOLD, LANES), f32),
             pltpu.VMEM((CHUNKS, GZ, 4, 5, HOLD, LANES), f32),
-            pltpu.VMEM((CHUNKS, 4, 5, ROWS, LANES), f32),
+            pltpu.VMEM((CHUNKS, 4, GROUPS, 5, HOLD, LANES), f32),
             pltpu.VMEM((2, 2, 8, 4, 5, HOLD, LANES), f32),
             pltpu.VMEM((HALF, NY), f32),
             pltpu.VMEM((HALF, NY), bf16),
             pltpu.VMEM((HALF, NY), bf16),
             pltpu.VMEM((NY, 5 * LANES), bf16),
             pltpu.VMEM((NY, 5 * LANES), bf16),
-            pltpu.VMEM((NZ // 2, 3 * NZ), bf16),
+            pltpu.VMEM((NZ, 2 * NZ), bf16),
             *[DMA((CHUNKS, 2))] * 4,
             *[DMA((CHUNKS, 3))] * 6,
             *[DMA((CHUNKS, 7))] * 2,
             *[DMA((CHUNKS, 2, 7))] * 2,
-            *[DMA((2, 7))] * 2,
+            *[DMA((2, 2, 7))] * 2,
             DMA((7,)),
             DMA((CHUNKS, 6)),
+            DMA((2, 5)),
         ],
         compiler_params=pltpu.CompilerParams(
             collective_id=0, has_side_effects=True, vmem_limit_bytes=62 << 20

time: 202 us -> 198 us (0.980)
  Pallas kernels: 201 us -> 197 us
    pallas_call x1, Pallas kernels: 197 us -> 193 us  [local(): pl.pallas_call(exchange, out_shape=(jax.ShapeDtypeStruct((2, 5, cells, LA...]
where the time goes in v4:
time: 198 us
  Pallas kernels  197 us (99%)
    pallas_call x1, Pallas kernels, local(): pl.pallas_call(exchange, out_shape=(jax.ShapeDtypeStruct((2, 5, cells, LA...  193 us
    pallas_call x1, Pallas kernels, local(): pl.pallas_call(join, out_shape=(jax.ShapeDtypeStruct((cells, CELLS), f32)...  4.46 us

profile of v4, /device:TPU:1, one launch (start us, length us, event | category | flops | bytes accessed | tf_op | source)
XLA Modules:
  0.0 197.7 jit_solution(16125452129196375729)
XLA Ops:
  0.6 192.5 %exchange.1 = (f32[2,5,1024,128]{3,2,1,0:T(8,128)}, f32[4,8,4,5,16,128]{5,4,3,2,1,0:T(8,128)}, f32[4,8,4,5,16,128]{5,4,3,2,1,0:T(8,128)}) custom-call(f32[1024,256]{1,0:T(8,128)} %bitcast.8, f32[3,1024,256]{2,1,0:T(8,128)} %bitcast.7, f32[1024,256]{1,0:T(8,128)} %bitcast.9, f32[1024,1024]{1,0:T(8,128)} %wall.1, f32[128,128]{1,0:T(8,128)} %span.1, ...), custom_call_target="tpu_custom_call" | custom-call | tf_op jit(solution)/shard_map/exchange/pallas_call | solution.py:441
  193.2 4.5 %join.1 = (f32[1024,256]{1,0:T(8,128)}, f32[3,1024,256]{2,1,0:T(8,128)}, f32[1024,256]{1,0:T(8,128)}) custom-call(f32[2,5,1024,128]{3,2,1,0:T(8,128)} %get-tuple-element.7.halves), custom_call_target="tpu_custom_call" | custom-call | tf_op jit(solution)/shard_map/join/pallas_call | solution.py:479

commit v5 on v4

--- a/solution.py
+++ b/solution.py
@@ -287,7 +287,7 @@
 
         for part in range(2):
 
-            @pl.loop(8 * part, 8 * part + 8)
+            @pl.loop(8 * part, 8 * part + 8, unroll=2)
             def _(r):
                 weight = damp[gy * ROWS + slot * HOLD + r]
                 c = []

time: 198 us -> 197 us (level)
  no operation moved by 1% of the time
where the time goes in v5:
time: 197 us
  Pallas kernels  196 us (99%)
    pallas_call x1, Pallas kernels, local(): pl.pallas_call(exchange, out_shape=(jax.ShapeDtypeStruct((2, 5, cells, LA...  192 us
    pallas_call x1, Pallas kernels, local(): pl.pallas_call(join, out_shape=(jax.ShapeDtypeStruct((cells, CELLS), f32)...  4.46 us

profile of v5, /device:TPU:1, one launch (start us, length us, event | category | flops | bytes accessed | tf_op | source)
XLA Modules:
  0.0 196.9 jit_solution(13492195378134467052)
XLA Ops:
  0.6 191.8 %exchange.1 = (f32[2,5,1024,128]{3,2,1,0:T(8,128)}, f32[4,8,4,5,16,128]{5,4,3,2,1,0:T(8,128)}, f32[4,8,4,5,16,128]{5,4,3,2,1,0:T(8,128)}) custom-call(f32[1024,256]{1,0:T(8,128)} %bitcast.8, f32[3,1024,256]{2,1,0:T(8,128)} %bitcast.7, f32[1024,256]{1,0:T(8,128)} %bitcast.9, f32[1024,1024]{1,0:T(8,128)} %wall.1, f32[128,128]{1,0:T(8,128)} %span.1, ...), custom_call_target="tpu_custom_call" | custom-call | tf_op jit(solution)/shard_map/exchange/pallas_call | solution.py:441
  192.4 4.5 %join.1 = (f32[1024,256]{1,0:T(8,128)}, f32[3,1024,256]{2,1,0:T(8,128)}, f32[1024,256]{1,0:T(8,128)}) custom-call(f32[2,5,1024,128]{3,2,1,0:T(8,128)} %get-tuple-element.7.halves), custom_call_target="tpu_custom_call" | custom-call | tf_op jit(solution)/shard_map/join/pallas_call | solution.py:479

commit v6 on v5

--- a/solution.py
+++ b/solution.py
@@ -354,8 +354,8 @@
     pass_far(2, 1)
     pass_near(3, 1)
     pass_far(3, 0)
+    pass_far(3, 1)
     derive_y(2)
-    pass_far(3, 1)
     derive_z(1)
     derive_y(3)
     add_y(0)

time: 197 us -> 197 us (level)
  no operation moved by 1% of the time
where the time goes in v6:
time: 197 us
  Pallas kernels  196 us (99%)
    pallas_call x1, Pallas kernels, local(): pl.pallas_call(exchange, out_shape=(jax.ShapeDtypeStruct((2, 5, cells, LA...  192 us
    pallas_call x1, Pallas kernels, local(): pl.pallas_call(join, out_shape=(jax.ShapeDtypeStruct((cells, CELLS), f32)...  4.46 us

profile of v6, /device:TPU:1, one launch (start us, length us, event | category | flops | bytes accessed | tf_op | source)
XLA Modules:
  0.0 196.9 jit_solution(15730527092325466759)
XLA Ops:
  0.6 191.8 %exchange.1 = (f32[2,5,1024,128]{3,2,1,0:T(8,128)}, f32[4,8,4,5,16,128]{5,4,3,2,1,0:T(8,128)}, f32[4,8,4,5,16,128]{5,4,3,2,1,0:T(8,128)}) custom-call(f32[1024,256]{1,0:T(8,128)} %bitcast.8, f32[3,1024,256]{2,1,0:T(8,128)} %bitcast.7, f32[1024,256]{1,0:T(8,128)} %bitcast.9, f32[1024,1024]{1,0:T(8,128)} %wall.1, f32[128,128]{1,0:T(8,128)} %span.1, ...), custom_call_target="tpu_custom_call" | custom-call | tf_op jit(solution)/shard_map/exchange/pallas_call | solution.py:441
  192.4 4.5 %join.1 = (f32[1024,256]{1,0:T(8,128)}, f32[3,1024,256]{2,1,0:T(8,128)}, f32[1024,256]{1,0:T(8,128)}) custom-call(f32[2,5,1024,128]{3,2,1,0:T(8,128)} %get-tuple-element.7.halves), custom_call_target="tpu_custom_call" | custom-call | tf_op jit(solution)/shard_map/join/pallas_call | solution.py:479
